TPU v7x, 128 devices: a whole 4x4x4 slice. The times are simulated.
128 devices in a mesh: seg: 8 (over z, core), sec: 16 (over y, x).
Axes of the slice: x: 4, y: 4, z: 4, core: 2. Of those that a mesh axis runs over, the one named last changes fastest.
Arguments:
- wave_block: bfloat16 [8, 4096, 128, 128], P('seg', 'sec'), may hold values from -6 to 6
- left_envs: bfloat16 [8, 128, 128, 24, 128], P('seg', 'sec'), may hold values from -0.109375 to 0.109375
- next_vectors: bfloat16 [8, 128, 128, 1024], P('seg', 'sec'), may hold values from -6 to 6
- site_weights: float32 [8, 24, 1024], P('seg'), may hold values from 0.5 to 2
- kept_counts: int32 [128], replicated, may hold values from 32 to 128
- slots_before: int32 [128], replicated, may hold values from 0 to 127, as said below
- slots_after: int32 [128], replicated, may hold values from 0 to 127, as said below
Outputs:
- mixed_out: bfloat16 [8, 128, 128, 1024], P('seg', 'sec')
Inputs may be any that keep to these rules, and one draw needn't show every extreme that they name: `slots_before`: A permutation of the sectors; device p of sec holds before-slots p * 8 to (p + 1) * 8 - 1. `slots_after`: A permutation of the sectors; device p of sec holds after-slots p * 8 to (p + 1) * 8 - 1. Of the sectors in one device's before-slots, at most 1 lie in any one device's after-slots, and exactly 1 for some pair of devices.
All inputs are finite; a program needn't handle non-finite values.
Results may differ from a plain program's by a relative error of at most 0.0058.
Values may be sent and summed in bfloat16 or wider, within the bound.
No kernel may reach another device: no remote copies, remote signals or barrier semaphores. Data moves between devices by JAX's collectives and lax.ppermute only.
A program may use at most 192 MiB of HBM per device.

v0:
```python
import jax
import jax.numpy as jnp
from jax import lax
from jax.sharding import PartitionSpec as P

CAP = 1


def passed_along(value, axis, steps):
    count = lax.axis_size(axis)
    first, last = (max(0, -steps), min(count, count - steps))
    return lax.ppermute(value, axis, [(source, source + steps) for source in range(first, last)])


def inverse_of(slots):
    length_of = slots.shape[0]
    indices = jnp.arange(length_of, dtype=jnp.int32)
    return jnp.sum(jnp.where(slots[:, None] == indices[None, :], indices[:, None], 0), axis=0)


def send_table(mine, inverse_dest, width, slot_cap, devices):
    target = jnp.take(inverse_dest, mine) // width
    positions = jnp.arange(mine.shape[0])
    same_target = (target[:, None] == target[None, :]) & (positions[None, :] < positions[:, None])
    rank_in = jnp.sum(same_target.astype(jnp.int32), axis=1)
    slot_index = target * slot_cap + rank_in
    return (jnp.arange(devices * slot_cap)[:, None] == slot_index[None, :]).astype(jnp.bfloat16)


def take_table(wanted, inverse_src, perm_src, inverse_dest, myself, width, slot_cap, devices):
    where_now = jnp.take(inverse_src, wanted)
    source = where_now // width
    place_in = where_now % width
    positions = jnp.arange(width)
    peer_sectors = jnp.take(perm_src, source[:, None] * width + positions[None, :])
    landing = jnp.take(inverse_dest, peer_sectors) // width
    earlier = (landing == myself) & (positions[None, :] < place_in[:, None])
    rank_in = jnp.sum(earlier.astype(jnp.int32), axis=1)
    slot_index = source * slot_cap + rank_in
    return (jnp.arange(devices * slot_cap)[None, :] == slot_index[:, None]).astype(jnp.bfloat16)


def select_rows(table, values):
    return jnp.dot(table, values, preferred_element_type=jnp.float32).astype(jnp.bfloat16)


def on_device(
    wave_block, left_envs, next_vectors, site_weights, kept_counts, slots_before, slots_after
):
    devices = lax.axis_size("sec")
    myself = lax.axis_index("sec")
    width = left_envs.shape[1]
    block_size = left_envs.shape[2]
    channels = left_envs.shape[3]
    total_rows = wave_block.shape[1] * devices
    local_rows = wave_block[0]
    previous = passed_along(left_envs[0], "seg", 1)
    columns = jnp.take(local_rows, slots_before, axis=1)
    gram_sum = lax.psum_scatter(
        jnp.einsum("rsa,rsb->sab", columns, columns, preferred_element_type=jnp.float32),
        "sec",
        scatter_dimension=0,
        tiled=True,
    )
    identity = jnp.eye(block_size, dtype=jnp.float32)
    gram_sum = gram_sum / total_rows + 0.1 * identity
    factor = jnp.linalg.cholesky(gram_sum)
    inverse = lax.linalg.triangular_solve(
        factor, jnp.broadcast_to(identity, gram_sum.shape), left_side=True, lower=True
    )
    mine_before = lax.dynamic_slice_in_dim(slots_before, myself * width, width)
    mine_after = lax.dynamic_slice_in_dim(slots_after, myself * width, width)
    kept_here = jnp.take(kept_counts, mine_before)
    keep_mask = (jnp.arange(block_size)[None, :] < kept_here[:, None]).astype(jnp.float32)
    inverse = inverse * keep_mask[:, :, None]
    channel_zero = (jnp.arange(channels) == 0).astype(jnp.float32)
    boundary = identity[:, None, :] * channel_zero[None, :, None]
    first_segment = lax.axis_index("seg") == 0
    left_env = jnp.where(first_segment, boundary[None], previous.astype(jnp.float32))
    truncated = jnp.einsum(
        "sab,sbwc,sdc->sawd", inverse, left_env, inverse, precision=lax.Precision.HIGHEST
    ).astype(jnp.bfloat16)
    weights = site_weights[0]
    inv_before = inverse_of(slots_before)
    inv_after = inverse_of(slots_after)
    own_vectors = next_vectors[0]
    out_table = send_table(mine_after, inv_before, width, CAP, devices)
    packed = select_rows(out_table, own_vectors.reshape(width, -1)).reshape(devices, CAP, -1)
    arrived = lax.all_to_all(packed, "sec", split_axis=0, concat_axis=0, tiled=True)
    in_table = take_table(
        mine_before, inv_after, slots_after, inv_before, myself, width, CAP, devices
    )
    vectors = select_rows(in_table, arrived.reshape(devices * CAP, -1)).reshape(own_vectors.shape)
    scaled = (vectors.astype(jnp.float32)[:, None] * weights[None, :, None, :]).astype(jnp.bfloat16)
    result = jnp.einsum(
        "sawd,swdc->sac", truncated, scaled, preferred_element_type=jnp.float32
    ).astype(jnp.bfloat16)
    back_table = send_table(mine_before, inv_after, width, CAP, devices)
    packed_back = select_rows(back_table, result.reshape(width, -1)).reshape(devices, CAP, -1)
    returned = lax.all_to_all(packed_back, "sec", split_axis=0, concat_axis=0, tiled=True)
    back_in = take_table(
        mine_after, inv_before, slots_before, inv_after, myself, width, CAP, devices
    )
    mixed_out = select_rows(back_in, returned.reshape(devices * CAP, -1)).reshape(own_vectors.shape)
    return mixed_out[None]


def solution(mesh):
    placed = (
        P("seg", "sec", None, None),
        P("seg", "sec", None, None, None),
        P("seg", "sec", None, None),
        P("seg", None, None),
        P(),
        P(),
        P(),
    )
    return jax.shard_map(
        on_device,
        mesh=mesh,
        in_specs=placed,
        out_specs=P("seg", "sec", None, None),
        check_vma=False,
    )
```

profile of v0, /device:TPU:32, one launch (start us, length us, event | category | flops | bytes accessed | tf_op | source)
XLA Modules:
  0.0 500.8 jit_solution(389100690471089327)
XLA Ops:
  6.5 0.7 compare_select_fusion.6
  7.2 0.7 compare_and_fusion.1
  7.9 12.0 %copy.81 = bf16[1,256,128,128]{3,1,2,0:T(8,128)(2,1)} copy(bf16[1,256,128,128]{3,2,1,0:T(8,128)(2,1)} %param.11) | data formatting | bytes 16777216 | tf_op args[0]
  19.9 10.0 %gather_fusion = bf16[128,256,128]{2,1,0:T(8,128)(2,1)} fusion(bf16[256,128,128]{2,0,1:T(8,128)(2,1)} %bitcast.57, s32[1024]{0:T(1024)S(1)} %pad_clamp_fusion.2), kind=kCustom, calls=%fused_computation.7 | custom fusion | bytes 16777728 | tf_op jit(solution)/shard_map/jit(_take)/gather | solution.py:58
  29.8 11.1 %fusion.7 = f32[128,128,128]{1,2,0:T(8,128)} fusion(bf16[128,256,128]{2,1,0:T(8,128)(2,1)} %gather_fusion, pred[128]{0:T(512)(128)(4,1)S(1)} %compare_and_fusion.1), kind=kOutput, calls=%fused_computation.21 | convolution fusion | flops 1077936128 | bytes 16777344 | tf_op jit(solution)/shard_map/rsa,rsb->sab/dot_general | solution.py:60
  41.0 2.1 collective-permute-start
  43.3 0.6 gather_fusion.4
  44.0 0.6 gather_fusion.5
  44.9 0.8 gather_fusion.6
  46.0 0.1 select_reduce_fusion.2
  46.1 0.8 gather_fusion.7
  47.0 0.6 gather_fusion.1
  48.0 0.8 gather_fusion.2
  49.1 0.8 gather_fusion.3
  49.9 1.2 copy.68
  51.1 0.2 convert_reduce_fusion
  51.3 0.2 convert_reduce_fusion.1
  51.5 3.2 fusion
  54.7 0.5 broadcast.323
  55.2 6.8 %reduce.6 = bf16[16,131072]{1,0:T(8,128)(2,1)} reduce(bf16[16,1,131072]{2,0,1:T(8,128)(2,1)} %fusion, bf16[]{:T(256)} %broadcast.323), dimensions={1}, to_apply=%copy.56.reduce_sub_computation | reduce | bytes 8388610 | tf_op jit(solution)/shard_map/reshape | solution.py:88
  62.0 6.7 %reshape.215 = bf16[16,2,65536]{2,1,0:T(2,128)(2,1)} reshape(bf16[16,131072]{1,0:T(8,128)(2,1)} %reduce.6) | data formatting | bytes 8388608
  68.6 7.6 %all-to-all-start = ((bf16[16,2,65536]{2,1,0:T(2,128)(2,1)}), bf16[16,2,65536]{2,1,0:T(2,128)(2,1)}, u32[]{:S(2)}, u32[]{:S(2)}) async-start(bf16[16,2,65536]{2,1,0:T(2,128)(2,1)} %reshape.215), calls=%async_computation.1 | async-start | bytes 8388608 | tf_op jit(solution)/shard_map/all_to_all | solution.py:89
  76.4 0.2 convert_reduce_fusion.2
  76.7 0.2 broadcast_multiply_fusion
  76.8 74.4 %all-to-all-done = bf16[16,2,65536]{2,1,0:T(2,128)(2,1)} async-done(((bf16[16,2,65536]{2,1,0:T(2,128)(2,1)}), bf16[16,2,65536]{2,1,0:T(2,128)(2,1)}, u32[]{:S(2)}, u32[]{:S(2)}) %all-to-all-start) | async-done | bytes 4194336 | tf_op jit(solution)/shard_map/all_to_all | solution.py:89
  151.3 12.3 %reshape.216 = bf16[16,1,131072]{2,1,0:T(2,128)(2,1)} reshape(bf16[16,2,65536]{2,1,0:T(2,128)(2,1)} %all-to-all-done) | data formatting | bytes 8388608
  163.6 8.1 %convolution_convert_fusion.3 = bf16[8,131072]{1,0:T(8,128)(2,1)S(1)} fusion(bf16[16,1,131072]{2,1,0:T(2,128)(2,1)} %reshape.216, s32[8]{0:T(128)S(1)} %get-tuple-element.18), kind=kOutput, calls=%fused_computation.13 | convolution fusion | flops 34603136 | bytes 6291488 | tf_op jit(solution)/shard_map/dot_general | solution.py:44
  171.7 3.3 copy.57
  175.0 8.5 %convert_select_fusion = f32[8,128,24,128]{3,2,1,0:T(8,128)} fusion(bf16[8,128,24,128]{3,2,1,0:T(8,128)(2,1)} %collective-permute-done, f32[128,24,128]{2,1,0:T(8,128)S(1)} %broadcast_multiply_fusion, pred[]{:T(512)S(6)} %eq.161), kind=kLoop, calls=%fused_computation.20 | loop fusion | flops 6291456 | bytes 20447232 | tf_op jit(solution)/shard_map/jit(_where)/select_n | solution.py:79
  183.5 1.1 multiply_add_fusion
  184.6 0.2 copy.52
  184.8 1.2 fusion.25
  186.0 93.8 %custom-call.7 = f32[8,128,128]{2,1,0:T(8,128)S(1)} custom-call(f32[8,128,128]{2,1,0:T(8,128)S(1)} %fusion.25), custom_call_target="Cholesky" | custom-call | tf_op jit(solution)/shard_map/jit(cholesky)/cholesky | solution.py:67
  279.8 0.1 compare_reduce_fusion
  279.9 0.1 select_bitcast_fusion
  280.1 78.8 %custom-call.8 = f32[8,1,128,128]{2,3,1,0:T(8,128)S(1)} custom-call(f32[8,1,128,128]{3,2,1,0:T(8,128)S(1)} %select_bitcast_fusion), custom_call_target="InvertDiagBlocksLowerTriangular" | custom-call | tf_op jit(solution)/shard_map/triangular_solve | solution.py:68
  358.9 1.0 fusion.23
  359.9 17.0 %fusion.5 = f32[8,24,128,128]{2,3,1,0:T(8,128)S(1)} fusion(f32[8,128,128,1]{2,1,3,0:T(8,128)S(1)} %fusion.23, f32[8,128,24,128]{3,2,1,0:T(8,128)} %convert_select_fusion), kind=kOutput, calls=%fused_computation.18 | convolution fusion | flops 4831838208 | bytes 25690112 | tf_op jit(solution)/shard_map/sab,sbwc,sdc->sawd/dot_general | solution.py:80
  376.9 11.2 %fusion.47 = bf16[8,24,128,128]{3,2,1,0:T(8,128)(2,1)S(1)} fusion(f32[8,24,128,128]{2,3,1,0:T(8,128)S(1)} %fusion.5, f32[8,128,128,1]{2,1,3,0:T(8,128)S(1)} %fusion.23), kind=kOutput, calls=%fused_computation.126 | convolution fusion | flops 4831838208 | bytes 19398656 | tf_op jit(solution)/shard_map/sab,sbwc,sdc->sawd/dot_general | solution.py:80
  388.1 7.7 %fusion.20 = bf16[1,8,128,1024]{3,2,1,0:T(8,128)(2,1)S(1)} fusion(f32[24,1024]{1,0:T(8,128)S(1)} %bitcast.63, f32[8,128,1024]{2,1,0:T(8,128)S(1)} %copy-done.4, bf16[8,24,128,128]{3,2,1,0:T(8,128)(2,1)S(1)} %fusion.47), kind=kOutput, calls=%fused_computation.34 | convolution fusion | flops 6493831168 | bytes 12681216 | tf_op jit(solution)/shard_map/sawd,swdc->sac/dot_general | solution.py:95
  395.9 1.2 copy.69
  397.0 3.2 fusion.1
  400.2 6.7 %reduce.7 = bf16[16,131072]{1,0:T(8,128)(2,1)} reduce(bf16[16,1,131072]{2,0,1:T(8,128)(2,1)} %fusion.1, bf16[]{:T(256)} %broadcast.323), dimensions={1}, to_apply=%copy.58.reduce_sub_computation | reduce | bytes 8388610 | tf_op jit(solution)/shard_map/reshape | solution.py:99
  406.9 6.7 %reshape.217 = bf16[16,2,65536]{2,1,0:T(2,128)(2,1)} reshape(bf16[16,131072]{1,0:T(8,128)(2,1)} %reduce.7) | data formatting | bytes 8388608
  413.6 57.1 %all_to_all.10 = bf16[16,2,65536]{2,1,0:T(2,128)(2,1)} all-to-all(bf16[16,2,65536]{2,1,0:T(2,128)(2,1)} %reshape.217), channel_id=1, replica_groups=mesh['seg'=8,'sec'=16] {'sec'}, dimensions={0} | all-to-all | bytes 8388608 | tf_op jit(solution)/shard_map/all_to_all | solution.py:100
  470.7 12.3 %reshape.218 = bf16[16,1,131072]{2,1,0:T(2,128)(2,1)} reshape(bf16[16,2,65536]{2,1,0:T(2,128)(2,1)} %all_to_all.10) | data formatting | bytes 8388608
  483.0 8.0 %convolution_convert_fusion.2 = bf16[8,131072]{1,0:T(8,128)(2,1)S(1)} fusion(bf16[16,1,131072]{2,1,0:T(2,128)(2,1)} %reshape.218, s32[8]{0:T(128)S(1)} %get-tuple-element.15), kind=kOutput, calls=%fused_computation.12 | convolution fusion | flops 34603136 | bytes 6291488 | tf_op jit(solution)/shard_map/dot_general | solution.py:44
  491.0 2.5 copy.59
  (54 shorter events, 1.9 us)
Async XLA Ops:
  6.5 37.4 %copy-start = (s32[128]{0:T(128)S(1)}, s32[128]{0:T(128)}, u32[]{:S(2)}) copy-start(s32[128]{0:T(128)} %param.15) | copy-start | bytes 1540
  6.5 177.0 %reduce-scatter.2.cloned.1.call-start = ((), (), s32[]{:S(2)}) async-start(), calls=%async_computation.3 | async-start | bytes 8912896 | tf_op jit(solution)/shard_map/reduce_scatter | solution.py:59
  40.9 2.2 copy-start.3
  40.9 2.3 copy-start.2
  41.0 134.1 %collective-permute-start = (bf16[8,128,24,128]{3,2,1,0:T(8,128)(2,1)}, bf16[8,128,24,128]{3,2,1,0:T(8,128)(2,1)}, u32[]{:S(2)}, u32[]{:S(2)}) collective-permute-start(bf16[8,128,24,128]{3,2,1,0:T(8,128)(2,1)} %bitcast.62), channel_id=1, source_target_pairs={{0,16},{16,32},{32,48},{48,64},{64,80},{80,96},{96,112},{1,17},{17... | collective-permute-start | bytes 18874376 | tf_op jit(solution)/shard_map/ppermute | solution.py:12
  46.1 3.8 copy-start.5
  68.6 82.7 %all-to-all-start = ((bf16[16,2,65536]{2,1,0:T(2,128)(2,1)}), bf16[16,2,65536]{2,1,0:T(2,128)(2,1)}, u32[]{:S(2)}, u32[]{:S(2)}) async-start(bf16[16,2,65536]{2,1,0:T(2,128)(2,1)} %reshape.215), calls=%async_computation.1 | async-start | bytes 8388608 | tf_op jit(solution)/shard_map/all_to_all | solution.py:89
  376.9 11.2 %copy-start.4 = (f32[8,128,1024]{2,1,0:T(8,128)S(1)}, f32[8,128,1024]{2,1,0:T(8,128)}, u32[]{:S(2)}) copy-start(f32[8,128,1024]{2,1,0:T(8,128)} %copy.57) | copy-start | bytes 12582916
  376.9 11.2 %copy-start.6 = (f32[1,24,1024]{2,1,0:T(8,128)S(1)}, f32[1,24,1024]{2,1,0:T(8,128)}, u32[]{:S(2)}) copy-start(f32[1,24,1024]{2,1,0:T(8,128)} %param.14) | copy-start | bytes 294916
  483.0 10.5 %copy-start.1 = (s32[128]{0:T(128)S(1)}, s32[128]{0:T(128)}, u32[]{:S(2)}) copy-start(s32[128]{0:T(128)} %param.15) | copy-start | bytes 1540
Sparse Core Ops, SparseCore 0:
  41.1 138.4 reduce-scatter.1
where the time goes:
time: 509 us; the launch traced here: 501 us
  other arithmetic  200 us (39%)
  local copies, waits for them, and re-layouts  74.5 us (15%)
  waiting for transfers between devices  74.5 us (15%)
  matrix products  70.5 us (14%)
  blocking collectives  57.1 us (11%)
  between operations  14.1 us (3%)
  starting transfers between devices  9.7 us (2%)
    another operation x3, other arithmetic, on_device(): factor = jnp.linalg.cholesky(gram_sum)  93.9 us
    another operation x3, other arithmetic, on_device(): lax.linalg.triangular_solve(factor, jnp.broadcast_to(identity, gram_sum.s...  78.9 us
    all_to_all x1, waiting for transfers between devices, on_device(): lax.all_to_all(packed, 'sec', split_axis=0, concat_axis=0, tiled=True)  74.4 us
    all_to_all x1, blocking collectives, on_device(): lax.all_to_all(packed_back, 'sec', split_axis=0, concat_axis=0, tiled=True)  57.1 us
    unnamed x21, local copies, waits for them, and re-layouts  52.3 us
    dot_general x2, matrix products, on_device(): jnp.einsum('sab,sbwc,sdc->sawd', inverse, left_env, inverse, precision=la...  28.2 us
    dot_general x4, matrix products, select_rows(): jnp.dot(table, values, preferred_element_type=jnp.float32)  22.5 us
    dot_general x1, matrix products, on_device(): jnp.einsum('rsa,rsb->sab', columns, columns, preferred_element_type=jnp.f...  11.1 us
  transfers between devices with their start and end apart: 3, of which 1 were waited for; matrix products, arithmetic and copies ran while one was open for 12% of the time, Pallas kernels for 0%

commit v1 on v0

v1 whole, which is shorter than its diff:
```python
import functools

import jax
import jax.numpy as jnp
from jax import lax
from jax.experimental import pallas as pl
from jax.experimental.pallas import tpu as pltpu
from jax.sharding import PartitionSpec as P

F32 = jnp.float32
BF16 = jnp.bfloat16


def whole(shape):
    return pl.BlockSpec(shape, lambda *_: (0,) * len(shape))


def passed_along(value, axis, steps):
    count = lax.axis_size(axis)
    first, last = (max(0, -steps), min(count, count - steps))
    return lax.ppermute(value, axis, [(source, source + steps) for source in range(first, last)])


def iota2(shape, axis):
    return lax.broadcasted_iota(jnp.int32, shape, axis)


def prologue_kernel(
    where_ref, before_ref, after_ref, kept_ref, vec_ref,
    packed_ref, place_ref, table_ref, inv_ref, sems,
):
    width = vec_ref.shape[0]
    total = before_ref.shape[0]
    base = where_ref[0] * width

    def invert(i, carry):
        place_ref[before_ref[i]] = i
        inv_ref[after_ref[i]] = i
        return carry

    lax.fori_loop(0, total, invert, 0)
    copies = []
    for j in range(width):
        to = place_ref[after_ref[base + j]] // width
        copy = pltpu.make_async_copy(vec_ref.at[j], packed_ref.at[to], sems.at[j])
        copy.start()
        copies.append(copy)
        sector = before_ref[base + j]
        table_ref[j] = inv_ref[sector] // width
        table_ref[width + j] = to
        table_ref[2 * width + j] = kept_ref[sector]
        table_ref[3 * width + j] = where_ref[1]
    for copy in copies:
        copy.wait()


def prologue(where, before, after, kept, vectors, devices):
    width, size, cols = vectors.shape
    total = before.shape[0]
    smem = pl.BlockSpec(memory_space=pltpu.SMEM)
    hbm = pl.BlockSpec(memory_space=pl.ANY)
    return pl.pallas_call(
        prologue_kernel,
        out_shape=(
            jax.ShapeDtypeStruct((devices, size, cols), vectors.dtype),
            jax.ShapeDtypeStruct((total,), jnp.int32),
            jax.ShapeDtypeStruct((4 * width,), jnp.int32),
        ),
        in_specs=[smem, smem, smem, smem, hbm],
        out_specs=(hbm, smem, smem),
        scratch_shapes=[pltpu.SMEM((total,), jnp.int32), pltpu.SemaphoreType.DMA((width,))],
        name="prologue",
    )(where, before, after, kept, vectors)


def gram_kernel(place_ref, x_ref, o_ref, diag_ref, *, width):
    step = pl.program_id(0)
    count, size = x_ref.shape[1:]
    half = size // 2
    turned = jnp.swapaxes(x_ref[...], 0, 1)
    row, lane = iota2((half, size), 0), iota2((half, size), 1)
    from_top = (lane >= half) & (row >= lane - half)
    on_diag = iota2((size, size), 0) == iota2((size, size), 1)
    for k in range(count):
        block = turned[k]
        full = lax.dot_general(
            block, block, (((0,), (0,)), ((), ())), preferred_element_type=F32
        )
        at = place_ref[step * count + k]
        packed = jnp.where(from_top, pltpu.roll(full[:half], half, 1), full[half:])
        start = pl.multiple_of((at % width) * half, half)
        o_ref[at // width, pl.ds(start, half), :] = packed.astype(BF16)
        diag_ref[pl.ds(at, 1), :] = jnp.sum(jnp.where(on_diag, full, 0.0), axis=0, keepdims=True)

    @pl.when(step == pl.num_programs(0) - 1)
    def _():
        for t in range(o_ref.shape[0]):
            exact = diag_ref[t * width : (t + 1) * width, :]
            high = exact.astype(BF16).astype(F32)
            both = jnp.concatenate([high, exact - high], axis=0)
            o_ref[t, width * half :, :] = both.astype(BF16)


def partial_grams(place, rows, width, count=32):
    length, sectors, size = rows.shape
    devices = sectors // width
    shape = (devices, width * (size // 2) + 2 * width, size)
    return pl.pallas_call(
        functools.partial(gram_kernel, width=width),
        out_shape=jax.ShapeDtypeStruct(shape, BF16),
        grid_spec=pltpu.PrefetchScalarGridSpec(
            num_scalar_prefetch=1,
            grid=(sectors // count,),
            in_specs=[pl.BlockSpec((length, count, size), lambda i, _: (0, i, 0))],
            out_specs=whole(shape),
            scratch_shapes=[pltpu.VMEM((sectors, size), F32)],
        ),
        name="gram",
    )(place, rows)


def split3(value):
    high = value.astype(BF16)
    rest = value - high.astype(F32)
    mid = rest.astype(BF16)
    low = (rest - mid.astype(F32)).astype(BF16)
    return high, mid, low


def factor_kernel(table_ref, g_ref, right_ref, left_ref, state_ref, *, total_rows):
    width, size, _ = state_ref.shape
    half = size // 2
    devices = g_ref.shape[0]
    summed = g_ref[0].astype(F32)
    for t in range(1, devices):
        summed = summed + g_ref[t].astype(F32)
    scale = 1.0 / total_rows
    diag = (summed[width * half : width * half + width] + summed[width * half + width :]) * scale
    packed = (summed[: width * half] * scale).reshape(width, half, size)
    lane = iota2((half, size), 1)
    row2, lane2 = iota2((size, size), 0), iota2((size, size), 1)
    for m in range(width):
        p = packed[m]
        turned = jnp.concatenate([p, p], axis=0).T
        top = jnp.where(lane >= half, turned[:half], pltpu.roll(turned[half:], half, 1))
        upper = jnp.concatenate([top, p], axis=0)
        both = jnp.where(lane2 > row2, upper, upper.T)
        state_ref[m] = jnp.where(lane2 == row2, diag[m : m + 1] + 0.1, both)

    lane8, sub8 = iota2((8, size), 1), iota2((8, size), 0)
    for r0 in range(0, size, 8):
        panel = state_ref[:, r0 : r0 + 8, :]
        for k in range(8):
            c = r0 + k
            col = panel[:, :, c : c + 1]
            pivot = panel[:, k : k + 1, c : c + 1]
            rk = lax.rsqrt(pivot)
            rk = rk * (1.5 - 0.5 * pivot * rk * rk)
            lead = jnp.where(lane8[:1] == c, rk, panel[:, k : k + 1, :] * rk)
            kept = jnp.where(lane8 == c, 0.0, panel) - (col * rk) * lead
            panel = jnp.where(sub8 > k, kept, jnp.where(sub8 == k, lead, panel))
        rest = r0 + 8
        panel = jnp.where((lane8 < rest) & (lane8 > r0 + sub8), 0.0, panel)
        state_ref[:, r0:rest, :] = panel
        if rest < size:
            h, m_, l = split3(panel)
            one = jnp.concatenate([h, h, h, m_, m_, l], axis=1)
            two = jnp.concatenate([h, m_, l, h, m_, h], axis=1)
            inside = (lane2[rest:] >= r0) & (lane2[rest:] < rest)
            for m in range(width):
                update = lax.dot_general(
                    one[m], two[m], (((0,), (0,)), ((), ())), preferred_element_type=F32
                )
                old = jnp.where(inside, 0.0, state_ref[m, rest:, :])
                state_ref[m, rest:, :] = old - update[rest:]

    for m in range(width):
        inverse = jnp.where(
            (lane2 <= row2) & (row2 < table_ref[2 * width + m]), state_ref[m], 0.0
        )
        high, low, _ = split3(inverse)
        left_ref[m] = jnp.concatenate([high, low, high], axis=1)
        high, low, _ = split3(inverse.T)
        right_ref[m] = jnp.concatenate([high, low], axis=1)


def inverse_factors(table, grams, width, total_rows):
    size = grams.shape[2]
    shapes = ((width, size, 2 * size), (width, size, 3 * size))
    return pl.pallas_call(
        functools.partial(factor_kernel, total_rows=total_rows),
        out_shape=tuple(jax.ShapeDtypeStruct(s, BF16) for s in shapes),
        grid_spec=pltpu.PrefetchScalarGridSpec(
            num_scalar_prefetch=1,
            grid=(1,),
            in_specs=[whole(grams.shape)],
            out_specs=tuple(whole(s) for s in shapes),
            scratch_shapes=[pltpu.VMEM((width, size, size), F32)],
        ),
        name="factor",
    )(table, grams)


def matvec_kernel(table_ref, v_ref, e_ref, w_ref, right_ref, left_ref, o_ref, *, width, group):
    channels, size = e_ref.shape[2:]
    v = v_ref[0]
    y = jnp.dot(right_ref[0], jnp.concatenate([v, v], axis=0), preferred_element_type=F32)
    env = jnp.swapaxes(e_ref[0], 0, 1)
    eye = (iota2((size, size), 0) == iota2((size, size), 1)).astype(BF16)
    first = table_ref[3 * width] == 0
    total = None
    for w in range(0, channels, group):
        blocks, scaled = [], []
        for u in range(w, w + group):
            block = env[u]
            blocks.append(jnp.where(first, eye if u == 0 else jnp.zeros_like(eye), block))
            scaled.append((y * w_ref[u : u + 1, :]).astype(BF16))
        part = jnp.dot(
            jnp.concatenate(blocks, axis=1),
            jnp.concatenate(scaled, axis=0),
            preferred_element_type=F32,
        )
        total = part if total is None else total + part
    high = total.astype(BF16)
    low = (total - high.astype(F32)).astype(BF16)
    o_ref[0] = jnp.dot(
        left_ref[0], jnp.concatenate([high, high, low], axis=0), preferred_element_type=F32
    ).astype(BF16)


def matvec(table, arrived, env, weights, right, left, group=4):
    width, size, channels, _ = env.shape
    devices, _, cols = arrived.shape
    at = pl.BlockSpec((1, size, cols), lambda i, t: (t[i], 0, 0))
    return pl.pallas_call(
        functools.partial(matvec_kernel, width=width, group=group),
        out_shape=jax.ShapeDtypeStruct((devices, size, cols), BF16),
        grid_spec=pltpu.PrefetchScalarGridSpec(
            num_scalar_prefetch=1,
            grid=(width,),
            in_specs=[
                at,
                pl.BlockSpec((1, size, channels, size), lambda i, t: (i, 0, 0, 0)),
                whole(weights.shape),
                pl.BlockSpec((1, size, 2 * size), lambda i, t: (i, 0, 0)),
                pl.BlockSpec((1, size, 3 * size), lambda i, t: (i, 0, 0)),
            ],
            out_specs=at,
        ),
        name="matvec",
    )(table, arrived, env, weights, right, left)


def gather_kernel(table_ref, x_ref, o_ref):
    o_ref[...] = x_ref[...]


def gathered(table, returned, width):
    devices, size, cols = returned.shape
    return pl.pallas_call(
        gather_kernel,
        out_shape=jax.ShapeDtypeStruct((width, size, cols), BF16),
        grid_spec=pltpu.PrefetchScalarGridSpec(
            num_scalar_prefetch=1,
            grid=(width,),
            in_specs=[pl.BlockSpec((1, size, cols), lambda j, t: (t[width + j], 0, 0))],
            out_specs=pl.BlockSpec((1, size, cols), lambda j, t: (j, 0, 0)),
        ),
        name="gather",
    )(table, returned)


def exchange(value):
    return lax.all_to_all(value, "sec", split_axis=0, concat_axis=0, tiled=True)


def on_device(
    wave_block, left_envs, next_vectors, site_weights, kept_counts, slots_before, slots_after
):
    devices = lax.axis_size("sec")
    width = left_envs.shape[1]
    previous = passed_along(left_envs[0], "seg", 1)
    where = jnp.stack([lax.axis_index("sec"), lax.axis_index("seg")]).astype(jnp.int32)
    packed, place, table = prologue(
        where, slots_before, slots_after, kept_counts, next_vectors[0], devices
    )
    arrived = exchange(packed)
    grams = exchange(partial_grams(place, wave_block[0], width))
    right, left = inverse_factors(table, grams, width, wave_block.shape[1] * devices)
    result = matvec(table, arrived, previous, site_weights[0], right, left)
    return gathered(table, exchange(result), width)[None]


def solution(mesh):
    placed = (
        P("seg", "sec", None, None),
        P("seg", "sec", None, None, None),
        P("seg", "sec", None, None),
        P("seg", None, None),
        P(),
        P(),
        P(),
    )
    return jax.shard_map(
        on_device,
        mesh=mesh,
        in_specs=placed,
        out_specs=P("seg", "sec", None, None),
        check_vma=False,
    )
```

time: 509 us -> 265 us (0.52); the launches traced: 501 us -> 265 us
  other arithmetic: 200 us -> 0.58 us
  Pallas kernels: 0 us -> 117 us
  local copies, waits for them, and re-layouts: 74.5 us -> 0 us
  matrix products: 70.5 us -> 0 us
  blocking collectives: 57.1 us -> 92.6 us
  waiting for transfers between devices: 74.5 us -> 47.7 us
  between operations: 14.1 us -> 0.03 us
    another operation x6 -> x1, other arithmetic: 173 us -> 0.58 us  [on_device(): jnp.stack([lax.axis_index('sec'), lax.axis_index('seg')]).astype(jnp.int32)]
    pallas_call x0 -> x5, Pallas kernels: none -> 117 us  [the longest x1 67.2 us: prologue(): pl.pallas_call(prologue_kernel, out_shape=(jax.ShapeDtypeStruct((devices,...]
    dot_general x8 -> x0, matrix products: 69.5 us -> none  [the longest x2 28.2 us: on_device(): jnp.einsum('sab,sbwc,sdc->sawd', inverse, left_env, inverse, precision=la...]
    unnamed x21 -> x0, local copies, waits for them, and re-layouts: 52.3 us -> none
    all_to_all x1 -> x2, blocking collectives: 57.1 us -> 92.6 us  [exchange(): return lax.all_to_all(value, 'sec', split_axis=0, concat_axis=0, tiled=True)]
    all_to_all x1, waiting for transfers between devices: 74.4 us -> 47.7 us  [exchange(): return lax.all_to_all(value, 'sec', split_axis=0, concat_axis=0, tiled=True)]
    gather x12 -> x0, local copies, waits for them, and re-layouts: 15.3 us -> none  [the longest x1 9.96 us: on_device(): columns = jnp.take(local_rows, slots_before, axis=1)]
    reshape x2 -> x0, other arithmetic: 13.5 us -> none  [the longest x1 6.76 us: on_device(): select_rows(out_table, own_vectors.reshape(width, -1))]
  transfers between devices with their start and end apart: 3 -> 2, of which waited for: 1 -> 1; matrix products, arithmetic and copies ran while one was open for 12% -> 0% of each run, Pallas kernels for 0% -> 36%
where the time goes in v1:
time: 265 us
  Pallas kernels  117 us (44%)
  blocking collectives  92.6 us (35%)
  waiting for transfers between devices  47.7 us (18%)
  starting transfers between devices  6.45 us (2%)
    all_to_all x2, blocking collectives, exchange(): return lax.all_to_all(value, 'sec', split_axis=0, concat_axis=0, tiled=True)  92.6 us
    pallas_call x1, Pallas kernels, prologue(): pl.pallas_call(prologue_kernel, out_shape=(jax.ShapeDtypeStruct((devices,...  67.2 us
    all_to_all x1, waiting for transfers between devices, exchange(): return lax.all_to_all(value, 'sec', split_axis=0, concat_axis=0, tiled=True)  47.7 us
    pallas_call x1, Pallas kernels, inverse_factors(): pl.pallas_call(functools.partial(factor_kernel, total_rows=total_rows), o...  18.3 us
    pallas_call x1, Pallas kernels, matvec(): pl.pallas_call(functools.partial(matvec_kernel, width=width, group=group)...  16.3 us
    pallas_call x1, Pallas kernels, partial_grams(): pl.pallas_call(functools.partial(gram_kernel, width=width), out_shape=jax...  9.14 us
    pallas_call x1, Pallas kernels, gathered(): pl.pallas_call(gather_kernel, out_shape=jax.ShapeDtypeStruct((width, size...  6.32 us
  transfers between devices with their start and end apart: 2, of which 1 were waited for; matrix products, arithmetic and copies ran while one was open for 0% of the time, Pallas kernels for 36%

profile of v1, /device:TPU:32, one launch (start us, length us, event | category | flops | bytes accessed | tf_op | source)
XLA Modules:
  0.0 264.7 jit_solution(7577654844665858091)
XLA Ops:
  0.0 1.9 collective-permute-start
  1.9 0.6 pad_add_fusion.where_ref
  2.5 67.2 %prologue.1 = (bf16[16,128,1024]{2,1,0:T(8,128)(2,1)}, s32[128]{0:T(128)}, s32[32]{0:T(128)}) custom-call(s32[2]{0:T(128)} %pad_add_fusion.where_ref, s32[128]{0:T(128)} %before_ref.1, s32[128]{0:T(128)} %after_ref.1, s32[128]{0:T(128)} %kept_ref.1, bf16[8,128,1024]{2,1,0:T(8,128)(2,1)} %bitcast.8), custom_call_target="tpu_custom_call" | custom-call | tf_op jit(solution)/shard_map/prologue/pallas_call | solution.py:62
  69.7 9.1 %gram.1 = bf16[16,528,128]{2,1,0:T(8,128)(2,1)} custom-call(s32[128]{0:T(128)} %get-tuple-element.12.place_ref, bf16[256,128,128]{2,1,0:T(8,128)(2,1)} %bitcast.7), custom_call_target="tpu_custom_call" | custom-call | tf_op jit(solution)/shard_map/gram/pallas_call | solution.py:108
  78.9 37.0 %all_to_all.15.g_ref = bf16[16,528,128]{2,1,0:T(8,128)(2,1)} all-to-all(bf16[16,528,128]{2,1,0:T(8,128)(2,1)} %gram.1), channel_id=1, replica_groups=mesh['seg'=8,'sec'=16] {'sec'}, dimensions={0} | all-to-all | bytes 4325376 | tf_op jit(solution)/shard_map/all_to_all | solution.py:274
  115.9 4.5 %all-to-all-start = ((bf16[16,128,1024]{2,1,0:T(8,128)(2,1)}), bf16[16,128,1024]{2,1,0:T(8,128)(2,1)}, u32[]{:S(2)}, u32[]{:S(2)}) async-start(bf16[16,128,1024]{2,1,0:T(8,128)(2,1)} %get-tuple-element.11), calls=%async_computation | async-start | bytes 8388608 | tf_op jit(solution)/shard_map/all_to_all | solution.py:274
  120.4 18.3 %factor.1 = (bf16[8,128,256]{2,1,0:T(8,128)(2,1)}, bf16[8,128,384]{2,1,0:T(8,128)(2,1)}) custom-call(s32[32]{0:T(128)} %get-tuple-element.10.table_ref, bf16[16,528,128]{2,1,0:T(8,128)(2,1)} %all_to_all.15.g_ref), custom_call_target="tpu_custom_call" | custom-call | tf_op jit(solution)/shard_map/factor/pallas_call | solution.py:190
  138.8 47.7 %all-to-all-done.v_ref = bf16[16,128,1024]{2,1,0:T(8,128)(2,1)} async-done(((bf16[16,128,1024]{2,1,0:T(8,128)(2,1)}), bf16[16,128,1024]{2,1,0:T(8,128)(2,1)}, u32[]{:S(2)}, u32[]{:S(2)}) %all-to-all-start) | async-done | bytes 4194336 | tf_op jit(solution)/shard_map/all_to_all | solution.py:274
  186.5 0.0 collective-permute-done.e_ref
  186.5 16.3 %matvec.1 = bf16[16,128,1024]{2,1,0:T(8,128)(2,1)} custom-call(s32[32]{0:T(128)} %get-tuple-element.10.table_ref, bf16[16,128,1024]{2,1,0:T(8,128)(2,1)} %all-to-all-done.v_ref, bf16[8,128,24,128]{3,2,1,0:T(8,128)(2,1)} %collective-permute-done.e_ref, f32[24,1024]{1,0:T(8,128)} %bitcast.9, bf16[8,128,256]{2,1,0:T(8,128)(2,1)} %get-tuple-element.13.right_ref, ...), custom_call_target="tpu_custom_call" | custom-call | tf_op jit(solution)/shard_map/matvec/pallas_call | solution.py:235
  202.8 55.6 %all_to_all.16.x_ref = bf16[16,128,1024]{2,1,0:T(8,128)(2,1)} all-to-all(bf16[16,128,1024]{2,1,0:T(8,128)(2,1)} %matvec.1), channel_id=1, replica_groups=mesh['seg'=8,'sec'=16] {'sec'}, dimensions={0} | all-to-all | bytes 8388608 | tf_op jit(solution)/shard_map/all_to_all | solution.py:274
  258.4 6.3 %gather.1 = bf16[8,128,1024]{2,1,0:T(8,128)(2,1)} custom-call(s32[32]{0:T(128)} %get-tuple-element.10.table_ref, bf16[16,128,1024]{2,1,0:T(8,128)(2,1)} %all_to_all.16.x_ref), custom_call_target="tpu_custom_call" | custom-call | tf_op jit(solution)/shard_map/gather/pallas_call | solution.py:260
Async XLA Ops:
  0.0 186.5 %collective-permute-start = (bf16[8,128,24,128]{3,2,1,0:T(8,128)(2,1)}, bf16[8,128,24,128]{3,2,1,0:T(8,128)(2,1)}, u32[]{:S(2)}, u32[]{:S(2)}) collective-permute-start(bf16[8,128,24,128]{3,2,1,0:T(8,128)(2,1)} %bitcast.10), channel_id=1, source_target_pairs={{0,16},{16,32},{32,48},{48,64},{64,80},{80,96},{96,112},{1,17},{17... | collective-permute-start | bytes 18874376 | tf_op jit(solution)/shard_map/ppermute | solution.py:21
  115.9 70.6 %all-to-all-start = ((bf16[16,128,1024]{2,1,0:T(8,128)(2,1)}), bf16[16,128,1024]{2,1,0:T(8,128)(2,1)}, u32[]{:S(2)}, u32[]{:S(2)}) async-start(bf16[16,128,1024]{2,1,0:T(8,128)(2,1)} %get-tuple-element.11), calls=%async_computation | async-start | bytes 8388608 | tf_op jit(solution)/shard_map/all_to_all | solution.py:274

commit v2 on v1

--- a/solution.py
+++ b/solution.py
@@ -7,6 +7,7 @@
 from jax.experimental.pallas import tpu as pltpu
 from jax.sharding import PartitionSpec as P
 
+
 F32 = jnp.float32
 BF16 = jnp.bfloat16
 
@@ -26,12 +27,13 @@
 
 
 def prologue_kernel(
-    where_ref, before_ref, after_ref, kept_ref, vec_ref,
-    packed_ref, place_ref, table_ref, inv_ref, sems,
+    where_ref, before_ref, after_ref, kept_ref, vec_ref, place_ref, table_ref, *rest
 ):
+    packed_refs, (inv_ref, sems) = rest[:-2], rest[-2:]
     width = vec_ref.shape[0]
     total = before_ref.shape[0]
     base = where_ref[0] * width
+    cols = packed_refs[0].shape[2]
 
     def invert(i, carry):
         place_ref[before_ref[i]] = i
@@ -39,38 +41,50 @@
         return carry
 
     lax.fori_loop(0, total, invert, 0)
-    copies = []
     for j in range(width):
-        to = place_ref[after_ref[base + j]] // width
-        copy = pltpu.make_async_copy(vec_ref.at[j], packed_ref.at[to], sems.at[j])
+        table_ref[width + j] = place_ref[after_ref[base + j]] // width
+    copies = [
+        pltpu.make_async_copy(
+            vec_ref.at[j, :, pl.ds(h * cols, cols)],
+            packed.at[table_ref[width + j]],
+            sems.at[h, j],
+        )
+        for h, packed in enumerate(packed_refs)
+        for j in range(width)
+    ]
+    for copy in copies:
         copy.start()
-        copies.append(copy)
+    for j in range(width):
         sector = before_ref[base + j]
         table_ref[j] = inv_ref[sector] // width
-        table_ref[width + j] = to
         table_ref[2 * width + j] = kept_ref[sector]
         table_ref[3 * width + j] = where_ref[1]
     for copy in copies:
         copy.wait()
 
 
-def prologue(where, before, after, kept, vectors, devices):
+def prologue(where, before, after, kept, vectors, devices, parts):
     width, size, cols = vectors.shape
     total = before.shape[0]
     smem = pl.BlockSpec(memory_space=pltpu.SMEM)
     hbm = pl.BlockSpec(memory_space=pl.ANY)
-    return pl.pallas_call(
+    packed = jax.ShapeDtypeStruct((devices, size, cols // parts), vectors.dtype)
+    place, table, *packs = pl.pallas_call(
         prologue_kernel,
         out_shape=(
-            jax.ShapeDtypeStruct((devices, size, cols), vectors.dtype),
             jax.ShapeDtypeStruct((total,), jnp.int32),
             jax.ShapeDtypeStruct((4 * width,), jnp.int32),
-        ),
-        in_specs=[smem, smem, smem, smem, hbm],
-        out_specs=(hbm, smem, smem),
-        scratch_shapes=[pltpu.SMEM((total,), jnp.int32), pltpu.SemaphoreType.DMA((width,))],
+        )
+        + (packed,) * parts,
+        in_specs=[smem, smem, smem, smem, pl.BlockSpec(memory_space=pltpu.VMEM)],
+        out_specs=(smem, smem) + (hbm,) * parts,
+        scratch_shapes=[
+            pltpu.SMEM((total,), jnp.int32),
+            pltpu.SemaphoreType.DMA((parts, width)),
+        ],
         name="prologue",
     )(where, before, after, kept, vectors)
+    return place, table, packs
 
 
 def gram_kernel(place_ref, x_ref, o_ref, diag_ref, *, width):
@@ -201,22 +215,25 @@
     )(table, grams)
 
 
-def matvec_kernel(table_ref, v_ref, e_ref, w_ref, right_ref, left_ref, o_ref, *, width, group):
-    channels, size = e_ref.shape[2:]
+def matvec_kernel(table_ref, v_ref, e_ref, w_ref, right_ref, left_ref, o_ref, *saved, width, group):
+    channels, size = w_ref.shape[0], v_ref.shape[1]
     v = v_ref[0]
     y = jnp.dot(right_ref[0], jnp.concatenate([v, v], axis=0), preferred_element_type=F32)
-    env = jnp.swapaxes(e_ref[0], 0, 1)
-    eye = (iota2((size, size), 0) == iota2((size, size), 1)).astype(BF16)
-    first = table_ref[3 * width] == 0
+    if saved:
+        env = jnp.swapaxes(e_ref[0], 0, 1)
+        eye = (iota2((size, size), 0) == iota2((size, size), 1)).astype(BF16)
+        first = table_ref[3 * width] == 0
     total = None
     for w in range(0, channels, group):
-        blocks, scaled = [], []
+        scaled = []
         for u in range(w, w + group):
-            block = env[u]
-            blocks.append(jnp.where(first, eye if u == 0 else jnp.zeros_like(eye), block))
+            if saved:
+                alone = eye if u == 0 else jnp.zeros_like(eye)
+                saved[0][0, :, u * size : (u + 1) * size] = jnp.where(first, alone, env[u])
             scaled.append((y * w_ref[u : u + 1, :]).astype(BF16))
+        here = saved[0] if saved else e_ref
         part = jnp.dot(
-            jnp.concatenate(blocks, axis=1),
+            here[0, :, w * size : (w + group) * size],
             jnp.concatenate(scaled, axis=0),
             preferred_element_type=F32,
         )
@@ -228,50 +245,81 @@
     ).astype(BF16)
 
 
-def matvec(table, arrived, env, weights, right, left, group=4):
-    width, size, channels, _ = env.shape
+def matvec(table, arrived, env, weights, right, left, part, group=4):
+    width, size, _ = right.shape
+    channels = weights.shape[0]
     devices, _, cols = arrived.shape
     at = pl.BlockSpec((1, size, cols), lambda i, t: (t[i], 0, 0))
+    wide = pl.BlockSpec((1, size, channels * size), lambda i, t: (i, 0, 0))
+    out_shape = [jax.ShapeDtypeStruct((devices, size, cols), BF16)]
+    out_specs = [at]
+    if part == 0:
+        out_shape.append(jax.ShapeDtypeStruct((width, size, channels * size), BF16))
+        out_specs.append(wide)
     return pl.pallas_call(
         functools.partial(matvec_kernel, width=width, group=group),
-        out_shape=jax.ShapeDtypeStruct((devices, size, cols), BF16),
+        out_shape=out_shape,
         grid_spec=pltpu.PrefetchScalarGridSpec(
             num_scalar_prefetch=1,
             grid=(width,),
             in_specs=[
                 at,
-                pl.BlockSpec((1, size, channels, size), lambda i, t: (i, 0, 0, 0)),
-                whole(weights.shape),
+                pl.BlockSpec((1, size, channels, size), lambda i, t: (i, 0, 0, 0))
+                if part == 0
+                else wide,
+                pl.BlockSpec((channels, cols), lambda i, t: (0, part)),
                 pl.BlockSpec((1, size, 2 * size), lambda i, t: (i, 0, 0)),
                 pl.BlockSpec((1, size, 3 * size), lambda i, t: (i, 0, 0)),
             ],
-            out_specs=at,
+            out_specs=out_specs,
         ),
-        name="matvec",
     )(table, arrived, env, weights, right, left)
 
 
-def gather_kernel(table_ref, x_ref, o_ref):
-    o_ref[...] = x_ref[...]
-
-
-def gathered(table, returned, width):
-    devices, size, cols = returned.shape
+def gather_kernel(table_ref, x_ref, *rest, part):
+    o_ref, buf_ref, sems = rest[-3:]
+    width, _, cols = buf_ref.shape
+    loads = [
+        pltpu.make_async_copy(x_ref.at[table_ref[width + j]], buf_ref.at[j], sems.at[0, j])
+        for j in range(width)
+    ]
+    stores = [
+        pltpu.make_async_copy(
+            buf_ref.at[j], o_ref.at[j, :, pl.ds(part * cols, cols)], sems.at[1, j]
+        )
+        for j in range(width)
+    ]
+    for load in loads:
+        load.start()
+    for load, store in zip(loads, stores):
+        load.wait()
+        store.start()
+    for store in stores:
+        store.wait()
+
+
+def gathered(table, returned, width, parts, part, filled):
+    _, size, cols = returned.shape
+    hbm = pl.BlockSpec(memory_space=pl.ANY)
+    more = [] if filled is None else [filled]
     return pl.pallas_call(
-        gather_kernel,
-        out_shape=jax.ShapeDtypeStruct((width, size, cols), BF16),
-        grid_spec=pltpu.PrefetchScalarGridSpec(
-            num_scalar_prefetch=1,
-            grid=(width,),
-            in_specs=[pl.BlockSpec((1, size, cols), lambda j, t: (t[width + j], 0, 0))],
-            out_specs=pl.BlockSpec((1, size, cols), lambda j, t: (j, 0, 0)),
-        ),
-        name="gather",
-    )(table, returned)
+        functools.partial(gather_kernel, part=part),
+        out_shape=jax.ShapeDtypeStruct((width, size, cols * parts), BF16),
+        in_specs=[pl.BlockSpec(memory_space=pltpu.SMEM), hbm] + [hbm] * len(more),
+        out_specs=hbm,
+        scratch_shapes=[
+            pltpu.VMEM((width, size, cols), BF16),
+            pltpu.SemaphoreType.DMA((2, width)),
+        ],
+        input_output_aliases={2: 0} if more else {},
+    )(table, returned, *more)
 
 
 def exchange(value):
     return lax.all_to_all(value, "sec", split_axis=0, concat_axis=0, tiled=True)
+
+
+PARTS = 2
 
 
 def on_device(
@@ -279,16 +327,26 @@
 ):
     devices = lax.axis_size("sec")
     width = left_envs.shape[1]
-    previous = passed_along(left_envs[0], "seg", 1)
+    env = passed_along(left_envs[0], "seg", 1)
     where = jnp.stack([lax.axis_index("sec"), lax.axis_index("seg")]).astype(jnp.int32)
-    packed, place, table = prologue(
-        where, slots_before, slots_after, kept_counts, next_vectors[0], devices
+    place, table, packs = prologue(
+        where, slots_before, slots_after, kept_counts, next_vectors[0], devices, PARTS
     )
-    arrived = exchange(packed)
-    grams = exchange(partial_grams(place, wave_block[0], width))
+    arrived = []
+    for h in range(PARTS):
+        arrived.append(exchange(packs[h]))
+    partial = partial_grams(place, wave_block[0], width)
+    grams = exchange(partial)
     right, left = inverse_factors(table, grams, width, wave_block.shape[1] * devices)
-    result = matvec(table, arrived, previous, site_weights[0], right, left)
-    return gathered(table, exchange(result), width)[None]
+    filled = None
+    results = []
+    for h in range(PARTS):
+        result, *saved = matvec(table, arrived[h], env, site_weights[0], right, left, h)
+        env = saved[0] if saved else env
+        results.append(exchange(result))
+    for h in range(PARTS):
+        filled = gathered(table, results[h], width, PARTS, h, filled)
+    return filled[None]
 
 
 def solution(mesh):

time: 265 us -> 199 us (0.75)
  blocking collectives: 92.6 us -> 34.7 us
  Pallas kernels: 117 us -> 64.2 us
  waiting for transfers between devices: 47.7 us -> 71.2 us
  starting transfers between devices: 6.45 us -> 23.6 us
  local copies, waits for them, and re-layouts: 0 us -> 3.99 us
    pallas_call x2 -> x3, Pallas kernels: 73.5 us -> 10.4 us  [the longest x2 5.5 us: gathered(): pl.pallas_call(functools.partial(gather_kernel, part=part), out_shape=jax...]
    all_to_all x2 -> x1, blocking collectives: 92.6 us -> 34.7 us  [exchange(): return lax.all_to_all(value, 'sec', split_axis=0, concat_axis=0, tiled=True)]
    all_to_all x1 -> x4, waiting for transfers between devices: 47.7 us -> 71.2 us  [exchange(): return lax.all_to_all(value, 'sec', split_axis=0, concat_axis=0, tiled=True)]
    all_to_all x1 -> x4, starting transfers between devices: 4.54 us -> 21.6 us  [exchange(): return lax.all_to_all(value, 'sec', split_axis=0, concat_axis=0, tiled=True)]
    pallas_call x1 -> x2, Pallas kernels: 16.3 us -> 26.2 us  [matvec(): pl.pallas_call(functools.partial(matvec_kernel, width=width, group=group)...]
    unnamed x0 -> x8, local copies, waits for them, and re-layouts: none -> 3.99 us
  transfers between devices with their start and end apart: 2 -> 5, of which waited for: 1 -> 3; matrix products, arithmetic and copies ran while one was open for 0% -> 0% of each run, Pallas kernels for 36% -> 31%
where the time goes in v2:
time: 199 us; the launch traced here: 198 us
  waiting for transfers between devices  71.2 us (36%)
  Pallas kernels  64.2 us (32%)
  blocking collectives  34.7 us (17%)
  starting transfers between devices  23.6 us (12%)
  local copies, waits for them, and re-layouts  3.99 us (2%)
    all_to_all x4, waiting for transfers between devices, exchange(): return lax.all_to_all(value, 'sec', split_axis=0, concat_axis=0, tiled=True)  71.2 us
    all_to_all x1, blocking collectives, exchange(): return lax.all_to_all(value, 'sec', split_axis=0, concat_axis=0, tiled=True)  34.7 us
    pallas_call x2, Pallas kernels, matvec(): pl.pallas_call(functools.partial(matvec_kernel, width=width, group=group)...  26.2 us
    all_to_all x4, starting transfers between devices, exchange(): return lax.all_to_all(value, 'sec', split_axis=0, concat_axis=0, tiled=True)  21.6 us
    pallas_call x1, Pallas kernels, inverse_factors(): pl.pallas_call(functools.partial(factor_kernel, total_rows=total_rows), o...  18.3 us
    pallas_call x1, Pallas kernels, partial_grams(): pl.pallas_call(functools.partial(gram_kernel, width=width), out_shape=jax...  9.22 us
    pallas_call x2, Pallas kernels, gathered(): pl.pallas_call(functools.partial(gather_kernel, part=part), out_shape=jax...  5.5 us
    pallas_call x1, Pallas kernels, prologue(): pl.pallas_call(prologue_kernel, out_shape=(jax.ShapeDtypeStruct((total,),...  4.85 us
  transfers between devices with their start and end apart: 5, of which 3 were waited for; matrix products, arithmetic and copies ran while one was open for 0% of the time, Pallas kernels for 31%

profile of v2, /device:TPU:32, one launch (start us, length us, event | category | flops | bytes accessed | tf_op | source)
XLA Modules:
  0.0 198.5 jit_solution(11063427967025447390)
XLA Ops:
  0.0 1.9 collective-permute-start
  1.9 0.7 pad_add_fusion.where_ref
  2.6 4.8 %prologue.1 = (s32[128]{0:T(128)}, s32[32]{0:T(128)}, bf16[16,128,512]{2,1,0:T(8,128)(2,1)}, bf16[16,128,512]{2,1,0:T(8,128)(2,1)}) custom-call(s32[2]{0:T(128)} %pad_add_fusion.where_ref, s32[128]{0:T(128)} %before_ref.1, s32[128]{0:T(128)} %after_ref.1, s32[128]{0:T(128)} %kept_ref.1, bf16[8,128,1024]{2,1,0:T(8,128)(2,1)} %bitcast.8), custom_call_target="tpu_custom_call" | custom-call | tf_op jit(solution)/shard_map/prologue/pallas_call | solution.py:72
  7.4 7.1 %all-to-all-start.1 = ((bf16[16,128,512]{2,1,0:T(8,128)(2,1)}), bf16[16,128,512]{2,1,0:T(8,128)(2,1)S(1)}, u32[]{:S(2)}, u32[]{:S(2)}) async-start(bf16[16,128,512]{2,1,0:T(8,128)(2,1)} %get-tuple-element.15), calls=%async_computation.1 | async-start | bytes 4194304 | tf_op jit(solution)/shard_map/all_to_all | solution.py:319
  14.5 9.2 %gram.1 = bf16[16,528,128]{2,1,0:T(8,128)(2,1)} custom-call(s32[128]{0:T(128)} %get-tuple-element.16.place_ref, bf16[256,128,128]{2,1,0:T(8,128)(2,1)} %bitcast.7), custom_call_target="tpu_custom_call" | custom-call | tf_op jit(solution)/shard_map/gram/pallas_call | solution.py:122
  23.7 24.9 %all-to-all-done.1.v_ref = bf16[16,128,512]{2,1,0:T(8,128)(2,1)S(1)} async-done(((bf16[16,128,512]{2,1,0:T(8,128)(2,1)}), bf16[16,128,512]{2,1,0:T(8,128)(2,1)S(1)}, u32[]{:S(2)}, u32[]{:S(2)}) %all-to-all-start.1) | async-done | bytes 2097184 | tf_op jit(solution)/shard_map/all_to_all | solution.py:319
  48.6 0.0 copy-start
  48.6 34.7 %all_to_all.25.g_ref = bf16[16,528,128]{2,1,0:T(8,128)(2,1)} all-to-all(bf16[16,528,128]{2,1,0:T(8,128)(2,1)} %gram.1), channel_id=1, replica_groups=mesh['seg'=8,'sec'=16] {'sec'}, dimensions={0} | all-to-all | bytes 4325376 | tf_op jit(solution)/shard_map/all_to_all | solution.py:319
  83.3 0.0 copy-done
  83.3 3.9 %all-to-all-start = ((bf16[16,128,512]{2,1,0:T(8,128)(2,1)}), bf16[16,128,512]{2,1,0:T(8,128)(2,1)S(1)}, u32[]{:S(2)}, u32[]{:S(2)}) async-start(bf16[16,128,512]{2,1,0:T(8,128)(2,1)} %get-tuple-element.14), calls=%async_computation | async-start | bytes 4194304 | tf_op jit(solution)/shard_map/all_to_all | solution.py:319
  87.2 18.3 %factor.1 = (bf16[8,128,256]{2,1,0:T(8,128)(2,1)}, bf16[8,128,384]{2,1,0:T(8,128)(2,1)}) custom-call(s32[32]{0:T(128)} %get-tuple-element.13.table_ref, bf16[16,528,128]{2,1,0:T(8,128)(2,1)} %all_to_all.25.g_ref), custom_call_target="tpu_custom_call" | custom-call | tf_op jit(solution)/shard_map/factor/pallas_call | solution.py:204
  105.5 0.0 collective-permute-done.e_ref
  105.5 13.9 %shard_map.73 = (bf16[16,128,512]{2,1,0:T(8,128)(2,1)}, bf16[8,128,3072]{2,1,0:T(8,128)(2,1)}) custom-call(s32[32]{0:T(128)} %get-tuple-element.13.table_ref, bf16[16,128,512]{2,1,0:T(8,128)(2,1)} %copy-done, bf16[8,128,24,128]{3,2,1,0:T(8,128)(2,1)} %collective-permute-done.e_ref, f32[24,1024]{1,0:T(8,128)} %bitcast.9, ...), custom_call_target="tpu_custom_call" | custom-call | tf_op jit(solution)/shard_map/pallas_call | solution.py:259
  119.4 0.0 all-to-all-done.v_ref
  119.4 0.0 copy-start.3
  119.4 1.3 copy-done.3
  120.8 7.0 %all-to-all-start.4 = ((bf16[16,128,512]{2,1,0:T(8,128)(2,1)}), bf16[16,128,512]{2,1,0:T(8,128)(2,1)S(1)}, u32[]{:S(2)}, u32[]{:S(2)}) async-start(bf16[16,128,512]{2,1,0:T(8,128)(2,1)} %get-tuple-element.20), calls=%async_computation.4 | async-start | bytes 4194304 | tf_op jit(solution)/shard_map/all_to_all | solution.py:319
  127.7 12.4 %shard_map.74 = bf16[16,128,512]{2,1,0:T(8,128)(2,1)} custom-call(s32[32]{0:T(128)} %get-tuple-element.13.table_ref, bf16[16,128,512]{2,1,0:T(8,128)(2,1)} %copy-done.3, bf16[8,128,3072]{2,1,0:T(8,128)(2,1)} %get-tuple-element.19.e_ref, f32[24,1024]{1,0:T(8,128)} %bitcast.10, bf16[8,128,256]{2,1,0:T(8,128)(2,1)} %get-tuple-element.17.right_ref, ...), custom_call_target="tpu_custom_call" | custom-call | tf_op jit(solution)/shard_map/pallas_call | solution.py:259
  140.1 18.4 %all-to-all-done.4.x_ref = bf16[16,128,512]{2,1,0:T(8,128)(2,1)S(1)} async-done(((bf16[16,128,512]{2,1,0:T(8,128)(2,1)}), bf16[16,128,512]{2,1,0:T(8,128)(2,1)S(1)}, u32[]{:S(2)}, u32[]{:S(2)}) %all-to-all-start.4) | async-done | bytes 2097184 | tf_op jit(solution)/shard_map/all_to_all | solution.py:319
  158.5 0.0 copy-start.2
  158.5 1.3 copy-done.2
  159.8 3.7 %all-to-all-start.3 = ((bf16[16,128,512]{2,1,0:T(8,128)(2,1)}), bf16[16,128,512]{2,1,0:T(8,128)(2,1)S(1)}, u32[]{:S(2)}, u32[]{:S(2)}) async-start(bf16[16,128,512]{2,1,0:T(8,128)(2,1)} %shard_map.74), calls=%async_computation.3 | async-start | bytes 4194304 | tf_op jit(solution)/shard_map/all_to_all | solution.py:319
  163.6 2.8 %shard_map.75.rest_0_ = bf16[8,128,1024]{2,1,0:T(8,128)(2,1)} custom-call(s32[32]{0:T(128)} %get-tuple-element.13.table_ref, bf16[16,128,512]{2,1,0:T(8,128)(2,1)} %copy-done.2), custom_call_target="tpu_custom_call" | custom-call | tf_op jit(solution)/shard_map/pallas_call | solution.py:305
  166.3 27.9 %all-to-all-done.3.x_ref = bf16[16,128,512]{2,1,0:T(8,128)(2,1)S(1)} async-done(((bf16[16,128,512]{2,1,0:T(8,128)(2,1)}), bf16[16,128,512]{2,1,0:T(8,128)(2,1)S(1)}, u32[]{:S(2)}, u32[]{:S(2)}) %all-to-all-start.3) | async-done | bytes 2097184 | tf_op jit(solution)/shard_map/all_to_all | solution.py:319
  194.2 0.0 copy-start.1
  194.2 1.3 copy-done.1
  195.5 2.8 %shard_map.76 = bf16[8,128,1024]{2,1,0:T(8,128)(2,1)} custom-call(s32[32]{0:T(128)} %get-tuple-element.13.table_ref, bf16[16,128,512]{2,1,0:T(8,128)(2,1)} %copy-done.1, bf16[8,128,1024]{2,1,0:T(8,128)(2,1)} %shard_map.75.rest_0_), custom_call_target="tpu_custom_call", output_to_operand_aliasing={{}: (2, {})} | custom-call | tf_op jit(solution)/shard_map/pallas_call | solution.py:305
Async XLA Ops:
  0.0 105.5 %collective-permute-start = (bf16[8,128,24,128]{3,2,1,0:T(8,128)(2,1)}, bf16[8,128,24,128]{3,2,1,0:T(8,128)(2,1)}, u32[]{:S(2)}, u32[]{:S(2)}) collective-permute-start(bf16[8,128,24,128]{3,2,1,0:T(8,128)(2,1)} %bitcast.11), channel_id=1, source_target_pairs={{0,16},{16,32},{32,48},{48,64},{64,80},{80,96},{96,112},{1,17},{17... | collective-permute-start | bytes 18874376 | tf_op jit(solution)/shard_map/ppermute | solution.py:22
  7.4 41.1 %all-to-all-start.1 = ((bf16[16,128,512]{2,1,0:T(8,128)(2,1)}), bf16[16,128,512]{2,1,0:T(8,128)(2,1)S(1)}, u32[]{:S(2)}, u32[]{:S(2)}) async-start(bf16[16,128,512]{2,1,0:T(8,128)(2,1)} %get-tuple-element.15), calls=%async_computation.1 | async-start | bytes 4194304 | tf_op jit(solution)/shard_map/all_to_all | solution.py:319
  48.6 34.7 %copy-start = (bf16[16,128,512]{2,1,0:T(8,128)(2,1)}, bf16[16,128,512]{2,1,0:T(8,128)(2,1)S(1)}, u32[]{:S(2)}) copy-start(bf16[16,128,512]{2,1,0:T(8,128)(2,1)S(1)} %all-to-all-done.1.v_ref) | copy-start | bytes 6291460
  83.3 36.1 %all-to-all-start = ((bf16[16,128,512]{2,1,0:T(8,128)(2,1)}), bf16[16,128,512]{2,1,0:T(8,128)(2,1)S(1)}, u32[]{:S(2)}, u32[]{:S(2)}) async-start(bf16[16,128,512]{2,1,0:T(8,128)(2,1)} %get-tuple-element.14), calls=%async_computation | async-start | bytes 4194304 | tf_op jit(solution)/shard_map/all_to_all | solution.py:319
  119.4 1.3 copy-start.3
  120.8 37.8 %all-to-all-start.4 = ((bf16[16,128,512]{2,1,0:T(8,128)(2,1)}), bf16[16,128,512]{2,1,0:T(8,128)(2,1)S(1)}, u32[]{:S(2)}, u32[]{:S(2)}) async-start(bf16[16,128,512]{2,1,0:T(8,128)(2,1)} %get-tuple-element.20), calls=%async_computation.4 | async-start | bytes 4194304 | tf_op jit(solution)/shard_map/all_to_all | solution.py:319
  158.5 1.3 copy-start.2
  159.8 34.4 %all-to-all-start.3 = ((bf16[16,128,512]{2,1,0:T(8,128)(2,1)}), bf16[16,128,512]{2,1,0:T(8,128)(2,1)S(1)}, u32[]{:S(2)}, u32[]{:S(2)}) async-start(bf16[16,128,512]{2,1,0:T(8,128)(2,1)} %shard_map.74), calls=%async_computation.3 | async-start | bytes 4194304 | tf_op jit(solution)/shard_map/all_to_all | solution.py:319
  194.2 1.3 copy-start.1

commit v3 on v1

v3 whole, which is shorter than its diff:
```python
import functools

import jax
import jax.numpy as jnp
from jax import lax
from jax.experimental import pallas as pl
from jax.experimental.pallas import tpu as pltpu
from jax.sharding import PartitionSpec as P


F32 = jnp.float32
BF16 = jnp.bfloat16
SIDE = 4
PARTS = 2


def passed_along(value, axis, steps):
    count = lax.axis_size(axis)
    first, last = (max(0, -steps), min(count, count - steps))
    return lax.ppermute(value, axis, [(source, source + steps) for source in range(first, last)])


def iota2(shape, axis):
    return lax.broadcasted_iota(jnp.int32, shape, axis)


def own_place(table_ref, width):
    mine = table_ref[3 * width]
    return mine // SIDE, mine % SIDE


def front_kernel(
    where_ref, before_ref, after_ref, kept_ref, vec_ref, x_ref, table_ref, *rest, width, parts
):
    packs, outs = rest[:parts], rest[parts : parts + 2 * SIDE]
    place_ref, inv_ref, vec_buf, o_ref, diag_ref, load_sem, pack_sems, sems = rest[parts + 2 * SIDE :]
    step = pl.program_id(0)
    last = pl.num_programs(0) - 1
    count, size = x_ref.shape[1:]
    half = size // 2
    each = width // 2
    cols = vec_buf.shape[2] // parts
    base = where_ref[0] * width
    mine_y, mine_x = where_ref[0] // SIDE, where_ref[0] % SIDE
    load = pltpu.make_async_copy(vec_ref, vec_buf, load_sem)

    def pack(j, h):
        return pltpu.make_async_copy(
            vec_buf.at[j, :, pl.ds(h * cols, cols)],
            packs[h].at[table_ref[width + j]],
            pack_sems.at[h, j],
        )

    @pl.when(step == 0)
    def _():
        load.start()
        diag_ref[...] = jnp.zeros_like(diag_ref)

        def invert(i, carry):
            place_ref[before_ref[i]] = i
            inv_ref[after_ref[i]] = i
            return carry

        lax.fori_loop(0, before_ref.shape[0], invert, 0)
        for j in range(width):
            sector = before_ref[base + j]
            table_ref[j] = inv_ref[sector] // width
            table_ref[width + j] = place_ref[after_ref[base + j]] // width
            table_ref[2 * width + j] = kept_ref[sector]
            table_ref[3 * width + j] = where_ref[j % 2]

    @pl.when(step == 1)
    def _():
        load.wait()
        for h in range(parts):
            for j in range(width):
                pack(j, h).start()

    turned = jnp.swapaxes(x_ref[...], 0, 1)
    row, lane = iota2((half, size), 0), iota2((half, size), 1)
    from_top = (lane >= half) & (row >= lane - half)
    on_diag = iota2((size, size), 0) == iota2((size, size), 1)
    for k in range(count):
        block = turned[k]
        full = lax.dot_general(
            block, block, (((0,), (0,)), ((), ())), preferred_element_type=F32
        )
        at = place_ref[step * count + k]
        to, slot = at // width, at % width
        colour, spot = slot // each, slot % each
        to_y, to_x = to // SIDE, to % SIDE
        along = jnp.where(colour == 0, to_x - mine_x + SIDE, to_y - mine_y + SIDE) % SIDE
        other = jnp.where(colour == 0, to_y, to_x)
        group = (colour * SIDE + along) * SIDE + other
        packed = jnp.where(from_top, pltpu.roll(full[:half], half, 1), full[half:])
        o_ref[group, pl.ds(pl.multiple_of(spot * half, half), half), :] = packed.astype(BF16)
        diag_ref[pl.ds(group * 8 + spot, 1), :] = jnp.sum(
            jnp.where(on_diag, full, 0.0), axis=0, keepdims=True
        )

    @pl.when(step == last)
    def _():
        copies = []
        for n, out in enumerate(outs):
            for m in range(n * SIDE, (n + 1) * SIDE):
                o_ref[m, each * half :, :] = two_halves(diag_ref[m * 8 : m * 8 + 8, :])
            copy = pltpu.make_async_copy(o_ref.at[pl.ds(n * SIDE, SIDE)], out, sems.at[n])
            copy.start()
            copies.append(copy)
        for h in range(parts):
            for j in range(width):
                pack(j, h).wait()
        for copy in copies:
            copy.wait()


def two_halves(exact):
    high = exact.astype(BF16).astype(F32)
    return jnp.concatenate([high, exact - high], axis=0).astype(BF16)


def front(where, before, after, kept, vectors, rows, parts, count=32):
    length, sectors, size = rows.shape
    width, _, cols = vectors.shape
    devices = sectors // width
    deep = (width // 2) * (size // 2) + 16
    hbm = pl.BlockSpec(memory_space=pl.ANY)
    table, *outs = pl.pallas_call(
        functools.partial(front_kernel, width=width, parts=parts),
        out_shape=[jax.ShapeDtypeStruct((4 * width,), jnp.int32)]
        + [jax.ShapeDtypeStruct((devices, size, cols // parts), BF16)] * parts
        + [jax.ShapeDtypeStruct((SIDE, deep, size), BF16)] * (2 * SIDE),
        grid_spec=pltpu.PrefetchScalarGridSpec(
            num_scalar_prefetch=4,
            grid=(sectors // count,),
            in_specs=[hbm, pl.BlockSpec((length, count, size), lambda i, *_: (0, i, 0))],
            out_specs=[pl.BlockSpec(memory_space=pltpu.SMEM)] + [hbm] * (parts + 2 * SIDE),
            scratch_shapes=[
                pltpu.SMEM((sectors,), jnp.int32),
                pltpu.SMEM((sectors,), jnp.int32),
                pltpu.VMEM(vectors.shape, BF16),
                pltpu.VMEM((2 * devices, deep, size), BF16),
                pltpu.VMEM((2 * devices * 8, size), F32),
                pltpu.SemaphoreType.DMA,
                pltpu.SemaphoreType.DMA((parts, width)),
                pltpu.SemaphoreType.DMA((2 * SIDE,)),
            ],
        ),
        name="front",
    )(where, before, after, kept, vectors, rows)
    return table, outs[:parts], outs[parts : parts + SIDE], outs[parts + SIDE :]


def added(parts):
    total = parts[0].astype(F32)
    for part in parts[1:]:
        total = total + part.astype(F32)
    return total


def sums_kernel(table_ref, *refs, width):
    mine = own_place(table_ref, width)
    for colour in range(2):
        ins = refs[colour * SIDE : (colour + 1) * SIDE]
        outs = refs[(2 + colour) * SIDE : (3 + colour) * SIDE]
        for along, out in enumerate(outs):
            at = (mine[colour] + along) % SIDE
            total = added([ref[at] for ref in ins])
            tail = total.shape[0] - 16
            out[:tail] = total[:tail].astype(BF16)
            out[tail:] = two_halves(total[tail : tail + 8] + total[tail + 8 :])


def axis_sums(table, first, second, width):
    _, deep, size = first[0].shape
    vmem = pl.BlockSpec(memory_space=pltpu.VMEM)
    outs = pl.pallas_call(
        functools.partial(sums_kernel, width=width),
        out_shape=[jax.ShapeDtypeStruct((deep, size), BF16)] * (2 * SIDE),
        in_specs=[pl.BlockSpec(memory_space=pltpu.SMEM)] + [vmem] * (2 * SIDE),
        out_specs=[vmem] * (2 * SIDE),
        name="sums",
    )(table, *first, *second)
    return outs[:SIDE], outs[SIDE:]


def turned_round(parts, axis):
    moved = [parts[0]]
    for along in range(1, SIDE):
        pairs = []
        for y in range(SIDE):
            for x in range(SIDE):
                to = (y, (x + along) % SIDE) if axis == "x" else ((y + along) % SIDE, x)
                pairs.append((y * SIDE + x, to[0] * SIDE + to[1]))
        moved.append(lax.ppermute(parts[along], "sec", pairs))
    return moved


def split3(value):
    high = value.astype(BF16)
    rest = value - high.astype(F32)
    mid = rest.astype(BF16)
    low = (rest - mid.astype(F32)).astype(BF16)
    return high, mid, low


def factor_kernel(table_ref, *refs, total_rows):
    right_ref, left_ref, state_ref = refs[-3:]
    width, size, _ = state_ref.shape
    half = size // 2
    each = width // 2
    scale = 1.0 / total_rows
    packed, diag = [], []
    for colour in range(2):
        total = added([ref[...] for ref in refs[colour * SIDE : (colour + 1) * SIDE]]) * scale
        tail = each * half
        exact = total[tail : tail + 8] + total[tail + 8 :]
        for m in range(each):
            packed.append(total[m * half : (m + 1) * half])
            diag.append(exact[m : m + 1])
    lane = iota2((half, size), 1)
    row2, lane2 = iota2((size, size), 0), iota2((size, size), 1)
    for m in range(width):
        p = packed[m]
        turned = jnp.concatenate([p, p], axis=0).T
        top = jnp.where(lane >= half, turned[:half], pltpu.roll(turned[half:], half, 1))
        upper = jnp.concatenate([top, p], axis=0)
        both = jnp.where(lane2 > row2, upper, upper.T)
        state_ref[m] = jnp.where(lane2 == row2, diag[m] + 0.1, both)

    lane8, sub8 = iota2((8, size), 1), iota2((8, size), 0)
    for r0 in range(0, size, 8):
        panel = state_ref[:, r0 : r0 + 8, :]
        for k in range(8):
            c = r0 + k
            col = panel[:, :, c : c + 1]
            pivot = panel[:, k : k + 1, c : c + 1]
            rk = lax.rsqrt(pivot)
            rk = rk * (1.5 - 0.5 * pivot * rk * rk)
            lead = jnp.where(lane8[:1] == c, rk, panel[:, k : k + 1, :] * rk)
            kept = jnp.where(lane8 == c, 0.0, panel) - (col * rk) * lead
            panel = jnp.where(sub8 > k, kept, jnp.where(sub8 == k, lead, panel))
        rest = r0 + 8
        panel = jnp.where((lane8 < rest) & (lane8 > r0 + sub8), 0.0, panel)
        state_ref[:, r0:rest, :] = panel
        if rest < size:
            h, m_, l = split3(panel)
            one = jnp.concatenate([h, h, h, m_, m_, l], axis=1)
            two = jnp.concatenate([h, m_, l, h, m_, h], axis=1)
            inside = (lane2[rest:] >= r0) & (lane2[rest:] < rest)
            for m in range(width):
                update = lax.dot_general(
                    one[m], two[m], (((0,), (0,)), ((), ())), preferred_element_type=F32
                )
                old = jnp.where(inside, 0.0, state_ref[m, rest:, :])
                state_ref[m, rest:, :] = old - update[rest:]

    for m in range(width):
        inverse = jnp.where(
            (lane2 <= row2) & (row2 < table_ref[2 * width + m]), state_ref[m], 0.0
        )
        high, low, _ = split3(inverse)
        left_ref[m] = jnp.concatenate([high, low, high], axis=1)
        high, low, _ = split3(inverse.T)
        right_ref[m] = jnp.concatenate([high, low], axis=1)


def inverse_factors(table, first, second, width, total_rows):
    size = first[0].shape[1]
    shapes = ((width, size, 2 * size), (width, size, 3 * size))
    vmem = pl.BlockSpec(memory_space=pltpu.VMEM)
    return pl.pallas_call(
        functools.partial(factor_kernel, total_rows=total_rows),
        out_shape=tuple(jax.ShapeDtypeStruct(s, BF16) for s in shapes),
        in_specs=[pl.BlockSpec(memory_space=pltpu.SMEM)] + [vmem] * (2 * SIDE),
        out_specs=(vmem, vmem),
        scratch_shapes=[pltpu.VMEM((width, size, size), F32)],
        name="factor",
    )(table, *first, *second)


def matvec_kernel(table_ref, v_ref, e_ref, w_ref, right_ref, left_ref, *rest, part, group):
    if part:
        _, o_ref, v_buf, wide_buf, y_buf, o_buf, sems = rest
    else:
        o_ref, wide_ref, v_buf, e_buf, wide_buf, y_buf, o_buf, sems = rest
    width, size, cols = v_buf.shape
    channels = w_ref.shape[0]
    span = pl.ds(part * cols, cols)
    copy = pltpu.make_async_copy
    v_in = [copy(v_ref.at[table_ref[i]], v_buf.at[i], sems.at[0, i]) for i in range(width)]
    e_to = wide_buf if part else e_buf
    e_in = [copy(e_ref.at[i], e_to.at[i], sems.at[1, i]) for i in range(width)]
    outs = [
        copy(o_buf.at[i], o_ref.at[table_ref[i], :, span], sems.at[2, i]) for i in range(width)
    ]
    for load in v_in + e_in:
        load.start()
    for i in range(width):
        v_in[i].wait()
        v = v_buf[i]
        y_buf[i] = jnp.dot(
            right_ref[i], jnp.concatenate([v, v], axis=0), preferred_element_type=F32
        )
    saves = []
    if not part:
        eye = (iota2((size, size), 0) == iota2((size, size), 1)).astype(BF16)
        first = table_ref[3 * width + 1] == 0

    def ready(i):
        e_in[i].wait()
        if part:
            return
        env = jnp.swapaxes(e_buf[i], 0, 1)
        for u in range(channels):
            alone = eye if u == 0 else jnp.zeros_like(eye)
            wide_buf[i, :, u * size : (u + 1) * size] = jnp.where(first, alone, env[u])
        saves.append(copy(wide_buf.at[i], wide_ref.at[i], sems.at[3, i]))
        saves[-1].start()

    def mixed(i):
        y = y_buf[i]
        total = None
        for w in range(0, channels, group):
            scaled = [
                (y * w_ref[u : u + 1, span]).astype(BF16) for u in range(w, w + group)
            ]
            piece = jnp.dot(
                wide_buf[i, :, w * size : (w + group) * size],
                jnp.concatenate(scaled, axis=0),
                preferred_element_type=F32,
            )
            total = piece if total is None else total + piece
        return total

    def finish(i, total):
        high = total.astype(BF16)
        low = (total - high.astype(F32)).astype(BF16)
        o_buf[i] = jnp.dot(
            left_ref[i], jnp.concatenate([high, high, low], axis=0), preferred_element_type=F32
        ).astype(BF16)
        outs[i].start()

    ready(0)
    before = None
    for i in range(width):
        if i + 1 < width:
            ready(i + 1)
        total = mixed(i)
        if i:
            finish(i - 1, before)
        before = total
    finish(width - 1, before)
    for out in outs + saves:
        out.wait()


def matvec(table, arrived, env, weights, right, left, part, filled, group=4):
    width, size, _ = right.shape
    channels, all_cols = weights.shape
    devices, _, cols = arrived.shape
    hbm = pl.BlockSpec(memory_space=pl.ANY)
    vmem = pl.BlockSpec(memory_space=pltpu.VMEM)
    out_shape = [jax.ShapeDtypeStruct((devices, size, all_cols), BF16)]
    wide = (width, size, channels * size)
    scratch = [pltpu.VMEM((width, size, cols), BF16)]
    if part == 0:
        out_shape.append(jax.ShapeDtypeStruct(wide, BF16))
        scratch.append(pltpu.VMEM(env.shape, BF16))
    scratch += [
        pltpu.VMEM(wide, BF16),
        pltpu.VMEM((width, size, cols), F32),
        pltpu.VMEM((width, size, cols), BF16),
        pltpu.SemaphoreType.DMA((4, width)),
    ]
    more = [] if part == 0 else [filled]
    return pl.pallas_call(
        functools.partial(matvec_kernel, part=part, group=group),
        out_shape=out_shape,
        in_specs=[pl.BlockSpec(memory_space=pltpu.SMEM), hbm, hbm, vmem, vmem, vmem]
        + [hbm] * len(more),
        out_specs=[hbm] * len(out_shape),
        scratch_shapes=scratch,
        input_output_aliases={6: 0} if more else {},
    )(table, arrived, env, weights, right, left, *more)


def gather_kernel(table_ref, x_ref, o_ref, buf_ref, sems):
    width = buf_ref.shape[0]
    loads = [
        pltpu.make_async_copy(x_ref.at[table_ref[width + j]], buf_ref.at[j], sems.at[0, j])
        for j in range(width)
    ]
    stores = [
        pltpu.make_async_copy(buf_ref.at[j], o_ref.at[j], sems.at[1, j]) for j in range(width)
    ]
    for load in loads:
        load.start()
    for load, store in zip(loads, stores):
        load.wait()
        store.start()
    for store in stores:
        store.wait()


def gathered(table, returned, width):
    _, size, cols = returned.shape
    hbm = pl.BlockSpec(memory_space=pl.ANY)
    shape = (width, size, cols)
    return pl.pallas_call(
        gather_kernel,
        out_shape=jax.ShapeDtypeStruct(shape, BF16),
        in_specs=[pl.BlockSpec(memory_space=pltpu.SMEM), hbm],
        out_specs=hbm,
        scratch_shapes=[pltpu.VMEM(shape, BF16), pltpu.SemaphoreType.DMA((2, width))],
        name="gather",
    )(table, returned)


def exchange(value):
    return lax.all_to_all(value, "sec", split_axis=0, concat_axis=0, tiled=True)


def on_device(
    wave_block, left_envs, next_vectors, site_weights, kept_counts, slots_before, slots_after
):
    width = left_envs.shape[1]
    total_rows = wave_block.shape[1] * lax.axis_size("sec")
    env = passed_along(left_envs[0], "seg", 1)
    where = jnp.stack([lax.axis_index("sec"), lax.axis_index("seg")]).astype(jnp.int32)
    table, packs, first, second = front(
        where, slots_before, slots_after, kept_counts, next_vectors[0], wave_block[0], PARTS
    )
    arrived = []
    for h in range(PARTS):
        arrived.append(exchange(packs[h]))
    first, second = turned_round(first, "x"), turned_round(second, "y")
    first, second = axis_sums(table, first, second, width)
    first, second = turned_round(first, "y"), turned_round(second, "x")
    right, left = inverse_factors(table, first, second, width, total_rows)
    result = None
    for h in range(PARTS):
        result, *wide = matvec(
            table, arrived[h], env, site_weights[0], right, left, h, result
        )
        env = wide[0] if wide else env
    returned = exchange(result)
    return gathered(table, returned, width)[None]


def solution(mesh):
    placed = (
        P("seg", "sec", None, None),
        P("seg", "sec", None, None, None),
        P("seg", "sec", None, None),
        P("seg", None, None),
        P(),
        P(),
        P(),
    )
    return jax.shard_map(
        on_device,
        mesh=mesh,
        in_specs=placed,
        out_specs=P("seg", "sec", None, None),
        check_vma=False,
    )
```

time: 265 us -> 228 us (0.86)
  Pallas kernels: 117 us -> 57.3 us
  starting transfers between devices: 6.45 us -> 31.5 us
  waiting for transfers between devices: 47.7 us -> 45 us
    pallas_call x4 -> x5, Pallas kernels: 98.9 us -> 40.2 us  [the longest x2 22.9 us: matvec(): pl.pallas_call(functools.partial(matvec_kernel, part=part, group=group),...]
    all_to_all x1, waiting for transfers between devices: 47.7 us -> 0.01 us  [exchange(): return lax.all_to_all(value, 'sec', split_axis=0, concat_axis=0, tiled=True)]
    ppermute x0 -> x12, waiting for transfers between devices: none -> 45 us  [turned_round(): moved.append(lax.ppermute(parts[along], 'sec', pairs))]
    ppermute x0 -> x12, starting transfers between devices: none -> 25.9 us  [turned_round(): moved.append(lax.ppermute(parts[along], 'sec', pairs))]
  transfers between devices with their start and end apart: 2 -> 14, of which waited for: 1 -> 5; matrix products, arithmetic and copies ran while one was open for 0% -> 0% of each run, Pallas kernels for 36% -> 19%
where the time goes in v3:
time: 228 us
  blocking collectives  91.1 us (40%)
  Pallas kernels  57.3 us (25%)
  waiting for transfers between devices  45 us (20%)
  starting transfers between devices  31.5 us (14%)
    all_to_all x2, blocking collectives, exchange(): return lax.all_to_all(value, 'sec', split_axis=0, concat_axis=0, tiled=True)  91.1 us
    ppermute x12, waiting for transfers between devices, turned_round(): moved.append(lax.ppermute(parts[along], 'sec', pairs))  45 us
    ppermute x12, starting transfers between devices, turned_round(): moved.append(lax.ppermute(parts[along], 'sec', pairs))  25.9 us
    pallas_call x2, Pallas kernels, matvec(): pl.pallas_call(functools.partial(matvec_kernel, part=part, group=group),...  22.9 us
    pallas_call x1, Pallas kernels, inverse_factors(): pl.pallas_call(functools.partial(factor_kernel, total_rows=total_rows), o...  17.1 us
    pallas_call x1, Pallas kernels, front(): pl.pallas_call(functools.partial(front_kernel, width=width, parts=parts),...  11.7 us
  transfers between devices with their start and end apart: 14, of which 5 were waited for; matrix products, arithmetic and copies ran while one was open for 0% of the time, Pallas kernels for 19%

profile of v3, /device:TPU:32, one launch (start us, length us, event | category | flops | bytes accessed | tf_op | source)
XLA Modules:
  0.0 227.9 jit_solution(2727290893043674977)
XLA Ops:
  0.0 1.9 collective-permute-start
  1.9 0.7 pad_add_fusion.where_ref
  2.6 11.7 %front.1 = (s32[32]{0:T(128)}, bf16[16,128,512]{2,1,0:T(8,128)(2,1)}, bf16[16,128,512]{2,1,0:T(8,128)(2,1)}, bf16[4,272,128]{2,1,0:T(8,128)(2,1)}, bf16[4,272,12...) custom-call(s32[2]{0:T(128)} %pad_add_fusion.where_ref, ...), custom_call_target="tpu_custom_call" | custom-call | tf_op jit(solution)/shard_map/front/pallas_call | solution.py:128
  14.3 0.0 copy-start.12
  14.3 36.4 %all_to_all.15.v_ref = bf16[16,128,512]{2,1,0:T(8,128)(2,1)} all-to-all(bf16[16,128,512]{2,1,0:T(8,128)(2,1)} %get-tuple-element.30), channel_id=1, replica_groups=mesh['seg'=8,'sec'=16] {'sec'}, dimensions={0} | all-to-all | bytes 4194304 | tf_op jit(solution)/shard_map/all_to_all | solution.py:421
  50.7 3.7 %all-to-all-start = ((bf16[16,128,512]{2,1,0:T(8,128)(2,1)}), bf16[16,128,512]{2,1,0:T(8,128)(2,1)S(1)}, u32[]{:S(2)}, u32[]{:S(2)}) async-start(bf16[16,128,512]{2,1,0:T(8,128)(2,1)} %get-tuple-element.29), calls=%async_computation | async-start | bytes 4194304 | tf_op jit(solution)/shard_map/all_to_all | solution.py:421
  54.4 0.0 copy-done.12
  54.4 1.9 collective-permute-start.1
  56.3 2.7 %collective-permute-start.2 = (bf16[4,272,128]{2,1,0:T(8,128)(2,1)}, bf16[4,272,128]{2,1,0:T(8,128)(2,1)S(1)}, u32[]{:S(2)}, u32[]{:S(2)}) collective-permute-start(bf16[4,272,128]{2,1,0:T(8,128)(2,1)} %get-tuple-element.33), channel_id=1, source_target_pairs={{0,2},{1,3},{2,0},{3,1},{4,6},{5,7},{6,4},{7,5},{8,10},{9,11},{10,... | collective-permute-start | bytes 835592 | tf_op jit(solution)/shard_map/ppermute | solution.py:195
  59.0 1.5 collective-permute-start.3
  60.5 1.5 collective-permute-start.4
  62.0 27.8 %collective-permute-done.1.refs_1_ = bf16[4,272,128]{2,1,0:T(8,128)(2,1)S(1)} collective-permute-done((bf16[4,272,128]{2,1,0:T(8,128)(2,1)S(1)}, bf16[4,272,128]{2,1,0:T(8,128)(2,1)S(1)}, u32[]{:S(2)}, u32[]{:S(2)}) %collective-permute-start.1) | collective-permute-done | bytes 278560 | tf_op jit(solution)/shard_map/ppermute | solution.py:195
  89.7 2.9 %collective-permute-start.5 = (bf16[4,272,128]{2,1,0:T(8,128)(2,1)}, bf16[4,272,128]{2,1,0:T(8,128)(2,1)S(1)}, u32[]{:S(2)}, u32[]{:S(2)}) collective-permute-start(bf16[4,272,128]{2,1,0:T(8,128)(2,1)} %get-tuple-element.37), channel_id=1, source_target_pairs={{0,8},{1,9},{2,10},{3,11},{4,12},{5,13},{6,14},{7,15},{8,0},{9,1},... | collective-permute-start | bytes 835592 | tf_op jit(solution)/shard_map/ppermute | solution.py:195
  92.6 7.4 %collective-permute-done.2.refs_2_ = bf16[4,272,128]{2,1,0:T(8,128)(2,1)S(1)} collective-permute-done((bf16[4,272,128]{2,1,0:T(8,128)(2,1)}, bf16[4,272,128]{2,1,0:T(8,128)(2,1)S(1)}, u32[]{:S(2)}, u32[]{:S(2)}) %collective-permute-start.2) | collective-permute-done | bytes 278560 | tf_op jit(solution)/shard_map/ppermute | solution.py:195
  100.0 1.7 collective-permute-start.6
  101.7 0.0 collective-permute-done.3.refs_3_
  101.7 0.0 collective-permute-done.4.refs_5_
  101.7 0.0 copy-start.4
  101.7 0.0 collective-permute-done.5.refs_6_
  101.7 0.0 copy-start.5
  101.8 6.8 %collective-permute-done.6.refs_7_ = bf16[4,272,128]{2,1,0:T(8,128)(2,1)} collective-permute-done((bf16[4,272,128]{2,1,0:T(8,128)(2,1)}, bf16[4,272,128]{2,1,0:T(8,128)(2,1)}, u32[]{:S(2)}, u32[]{:S(2)}) %collective-permute-start.6) | collective-permute-done | bytes 278560 | tf_op jit(solution)/shard_map/ppermute | solution.py:195
  108.6 0.0 copy-done.1
  108.6 0.0 copy-done.2
  108.6 0.0 copy-done.3
  108.6 0.0 copy-done.4
  108.6 2.5 %sums.1 = (bf16[272,128]{1,0:T(8,128)(2,1)}, bf16[272,128]{1,0:T(8,128)(2,1)}, bf16[272,128]{1,0:T(8,128)(2,1)}, bf16[272,128]{1,0:T(8,128)(2,1)}, bf16[272,128]...) custom-call(s32[32]{0:T(128)} %get-tuple-element.28.table_ref, ...), custom_call_target="tpu_custom_call" | custom-call | tf_op jit(solution)/shard_map/sums/pallas_call | solution.py:177
  111.2 1.1 collective-permute-start.7
  112.3 3.3 %collective-permute-start.8 = (bf16[272,128]{1,0:T(8,128)(2,1)}, bf16[272,128]{1,0:T(8,128)(2,1)S(1)}, u32[]{:S(2)}, u32[]{:S(2)}) collective-permute-start(bf16[272,128]{1,0:T(8,128)(2,1)} %get-tuple-element.41), channel_id=1, source_target_pairs={{0,8},{1,9},{2,10},{3,11},{4,12},{5,13},{6,14},{7,15},{8,0},{9,1},... | collective-permute-start | bytes 208904 | tf_op jit(solution)/shard_map/ppermute | solution.py:195
  115.6 1.1 collective-permute-start.9
  116.7 3.0 %collective-permute-start.10 = (bf16[272,128]{1,0:T(8,128)(2,1)}, bf16[272,128]{1,0:T(8,128)(2,1)S(1)}, u32[]{:S(2)}, u32[]{:S(2)}) collective-permute-start(bf16[272,128]{1,0:T(8,128)(2,1)} %get-tuple-element.44), channel_id=1, source_target_pairs={{0,1},{1,2},{2,3},{3,0},{4,5},{5,6},{6,7},{7,4},{8,9},{9,10},{10,1... | collective-permute-start | bytes 208904 | tf_op jit(solution)/shard_map/ppermute | solution.py:195
  119.7 0.0 collective-permute-done.7.refs_1_
  119.7 3.8 %collective-permute-start.11 = (bf16[272,128]{1,0:T(8,128)(2,1)}, bf16[272,128]{1,0:T(8,128)(2,1)S(1)}, u32[]{:S(2)}, u32[]{:S(2)}) collective-permute-start(bf16[272,128]{1,0:T(8,128)(2,1)} %get-tuple-element.45), channel_id=1, source_target_pairs={{0,2},{1,3},{2,0},{3,1},{4,6},{5,7},{6,4},{7,5},{8,10},{9,11},{10,... | collective-permute-start | bytes 208904 | tf_op jit(solution)/shard_map/ppermute | solution.py:195
  123.5 0.0 collective-permute-done.8.refs_2_
  123.5 1.5 collective-permute-start.12
  125.0 0.0 collective-permute-done.9.refs_3_
  125.0 0.0 collective-permute-done.10.refs_5_
  125.0 1.0 collective-permute-done.11.refs_6_
  126.0 2.0 collective-permute-done.12.refs_7_
  128.1 0.6 copy-done.11
  128.7 17.1 %factor.1 = (bf16[8,128,256]{2,1,0:T(8,128)(2,1)}, bf16[8,128,384]{2,1,0:T(8,128)(2,1)}) custom-call(s32[32]{0:T(128)} %get-tuple-element.28.table_ref, bf16[272,128]{1,0:T(8,128)(2,1)} %get-tuple-element.39.refs_0_, bf16[272,128]{1,0:T(8,128)(2,1)} %copy-done.6, bf16[272,128]{1,0:T(8,128)(2,1)} %copy-done.7, bf16[272,128]{1,0:T(8,128)(2,1)} %copy-done.8, ...), custom_call_target="tpu_custom_call" | custom-call | tf_op jit(solution)/shard_map/factor/pallas_call | solution.py:272
  145.8 0.0 collective-permute-done.e_ref
  145.8 13.0 %shard_map.73 = (bf16[16,128,1024]{2,1,0:T(8,128)(2,1)}, bf16[8,128,3072]{2,1,0:T(8,128)(2,1)}) custom-call(s32[32]{0:T(128)} %get-tuple-element.28.table_ref, bf16[16,128,512]{2,1,0:T(8,128)(2,1)} %all_to_all.15.v_ref, bf16[8,128,24,128]{3,2,1,0:T(8,128)(2,1)} %collective-permute-done.e_ref, f32[24,1024]{1,0:T(8,128)} %bitcast.9, ...), custom_call_target="tpu_custom_call" | custom-call | tf_op jit(solution)/shard_map/pallas_call | solution.py:377
  158.8 0.0 all-to-all-done.v_ref
  158.8 0.0 copy-start
  158.8 1.3 copy-done
  160.2 9.9 %shard_map.74 = bf16[16,128,1024]{2,1,0:T(8,128)(2,1)} custom-call(s32[32]{0:T(128)} %get-tuple-element.28.table_ref, bf16[16,128,512]{2,1,0:T(8,128)(2,1)} %copy-done, bf16[8,128,3072]{2,1,0:T(8,128)(2,1)} %get-tuple-element.49.e_ref, f32[24,1024]{1,0:T(8,128)} %bitcast.10, ...), custom_call_target="tpu_custom_call", output_to_operand_aliasing={{}: (6, {})} | custom-call | tf_op jit(solution)/shard_map/pallas_call | solution.py:377
  170.0 54.7 %all_to_all.16.x_ref = bf16[16,128,1024]{2,1,0:T(8,128)(2,1)} all-to-all(bf16[16,128,1024]{2,1,0:T(8,128)(2,1)} %shard_map.74), channel_id=1, replica_groups=mesh['seg'=8,'sec'=16] {'sec'}, dimensions={0} | all-to-all | bytes 8388608 | tf_op jit(solution)/shard_map/all_to_all | solution.py:421
  224.7 3.1 %gather.1 = bf16[8,128,1024]{2,1,0:T(8,128)(2,1)} custom-call(s32[32]{0:T(128)} %get-tuple-element.28.table_ref, bf16[16,128,1024]{2,1,0:T(8,128)(2,1)} %all_to_all.16.x_ref), custom_call_target="tpu_custom_call" | custom-call | tf_op jit(solution)/shard_map/gather/pallas_call | solution.py:410
  (15 shorter events, 0.0 us)
Async XLA Ops:
  0.0 145.8 %collective-permute-start = (bf16[8,128,24,128]{3,2,1,0:T(8,128)(2,1)}, bf16[8,128,24,128]{3,2,1,0:T(8,128)(2,1)}, u32[]{:S(2)}, u32[]{:S(2)}) collective-permute-start(bf16[8,128,24,128]{3,2,1,0:T(8,128)(2,1)} %bitcast.11), channel_id=1, source_target_pairs={{0,16},{16,32},{32,48},{48,64},{64,80},{80,96},{96,112},{1,17},{17... | collective-permute-start | bytes 18874376 | tf_op jit(solution)/shard_map/ppermute | solution.py:20
  14.3 40.2 %copy-start.12 = (bf16[4,272,128]{2,1,0:T(8,128)(2,1)S(1)}, bf16[4,272,128]{2,1,0:T(8,128)(2,1)}, u32[]{:S(2)}) copy-start(bf16[4,272,128]{2,1,0:T(8,128)(2,1)} %get-tuple-element.32) | copy-start | bytes 835588
  50.7 108.1 %all-to-all-start = ((bf16[16,128,512]{2,1,0:T(8,128)(2,1)}), bf16[16,128,512]{2,1,0:T(8,128)(2,1)S(1)}, u32[]{:S(2)}, u32[]{:S(2)}) async-start(bf16[16,128,512]{2,1,0:T(8,128)(2,1)} %get-tuple-element.29), calls=%async_computation | async-start | bytes 4194304 | tf_op jit(solution)/shard_map/all_to_all | solution.py:421
  54.4 35.3 %collective-permute-start.1 = (bf16[4,272,128]{2,1,0:T(8,128)(2,1)S(1)}, bf16[4,272,128]{2,1,0:T(8,128)(2,1)S(1)}, u32[]{:S(2)}, u32[]{:S(2)}) collective-permute-start(bf16[4,272,128]{2,1,0:T(8,128)(2,1)S(1)} %copy-done.12), channel_id=1, source_target_pairs={{0,1},{1,2},{2,3},{3,0},{4,5},{5,6},{6,7},{7,4},{8,9},{9,10},{10,1... | collective-permute-start | bytes 835592 | tf_op jit(solution)/shard_map/ppermute | solution.py:195
  56.3 43.7 %collective-permute-start.2 = (bf16[4,272,128]{2,1,0:T(8,128)(2,1)}, bf16[4,272,128]{2,1,0:T(8,128)(2,1)S(1)}, u32[]{:S(2)}, u32[]{:S(2)}) collective-permute-start(bf16[4,272,128]{2,1,0:T(8,128)(2,1)} %get-tuple-element.33), channel_id=1, source_target_pairs={{0,2},{1,3},{2,0},{3,1},{4,6},{5,7},{6,4},{7,5},{8,10},{9,11},{10,... | collective-permute-start | bytes 835592 | tf_op jit(solution)/shard_map/ppermute | solution.py:195
  59.0 42.7 %collective-permute-start.3 = (bf16[4,272,128]{2,1,0:T(8,128)(2,1)}, bf16[4,272,128]{2,1,0:T(8,128)(2,1)S(1)}, u32[]{:S(2)}, u32[]{:S(2)}) collective-permute-start(bf16[4,272,128]{2,1,0:T(8,128)(2,1)} %get-tuple-element.34), channel_id=1, source_target_pairs={{0,3},{1,0},{2,1},{3,2},{4,7},{5,4},{6,5},{7,6},{8,11},{9,8},{10,9... | collective-permute-start | bytes 835592 | tf_op jit(solution)/shard_map/ppermute | solution.py:195
  60.5 41.3 %collective-permute-start.4 = (bf16[4,272,128]{2,1,0:T(8,128)(2,1)}, bf16[4,272,128]{2,1,0:T(8,128)(2,1)S(1)}, u32[]{:S(2)}, u32[]{:S(2)}) collective-permute-start(bf16[4,272,128]{2,1,0:T(8,128)(2,1)} %get-tuple-element.36), channel_id=1, source_target_pairs={{0,4},{1,5},{2,6},{3,7},{4,8},{5,9},{6,10},{7,11},{8,12},{9,13},{1... | collective-permute-start | bytes 835592 | tf_op jit(solution)/shard_map/ppermute | solution.py:195
  89.7 18.9 %copy-start.1 = (bf16[4,272,128]{2,1,0:T(8,128)(2,1)}, bf16[4,272,128]{2,1,0:T(8,128)(2,1)S(1)}, u32[]{:S(2)}) copy-start(bf16[4,272,128]{2,1,0:T(8,128)(2,1)S(1)} %collective-permute-done.1.refs_1_) | copy-start | bytes 835588
  89.7 12.0 %collective-permute-start.5 = (bf16[4,272,128]{2,1,0:T(8,128)(2,1)}, bf16[4,272,128]{2,1,0:T(8,128)(2,1)S(1)}, u32[]{:S(2)}, u32[]{:S(2)}) collective-permute-start(bf16[4,272,128]{2,1,0:T(8,128)(2,1)} %get-tuple-element.37), channel_id=1, source_target_pairs={{0,8},{1,9},{2,10},{3,11},{4,12},{5,13},{6,14},{7,15},{8,0},{9,1},... | collective-permute-start | bytes 835592 | tf_op jit(solution)/shard_map/ppermute | solution.py:195
  100.0 8.6 %copy-start.2 = (bf16[4,272,128]{2,1,0:T(8,128)(2,1)}, bf16[4,272,128]{2,1,0:T(8,128)(2,1)S(1)}, u32[]{:S(2)}) copy-start(bf16[4,272,128]{2,1,0:T(8,128)(2,1)S(1)} %collective-permute-done.2.refs_2_) | copy-start | bytes 835588
  100.0 8.6 %collective-permute-start.6 = (bf16[4,272,128]{2,1,0:T(8,128)(2,1)}, bf16[4,272,128]{2,1,0:T(8,128)(2,1)}, u32[]{:S(2)}, u32[]{:S(2)}) collective-permute-start(bf16[4,272,128]{2,1,0:T(8,128)(2,1)} %get-tuple-element.38), channel_id=1, source_target_pairs={{0,12},{1,13},{2,14},{3,15},{4,0},{5,1},{6,2},{7,3},{8,4},{9,5},{1... | collective-permute-start | bytes 835592 | tf_op jit(solution)/shard_map/ppermute | solution.py:195
  101.7 6.9 %copy-start.3 = (bf16[4,272,128]{2,1,0:T(8,128)(2,1)}, bf16[4,272,128]{2,1,0:T(8,128)(2,1)S(1)}, u32[]{:S(2)}) copy-start(bf16[4,272,128]{2,1,0:T(8,128)(2,1)S(1)} %collective-permute-done.3.refs_3_) | copy-start | bytes 835588
  101.7 6.9 %copy-start.4 = (bf16[4,272,128]{2,1,0:T(8,128)(2,1)}, bf16[4,272,128]{2,1,0:T(8,128)(2,1)S(1)}, u32[]{:S(2)}) copy-start(bf16[4,272,128]{2,1,0:T(8,128)(2,1)S(1)} %collective-permute-done.4.refs_5_) | copy-start | bytes 835588
  101.7 6.9 %copy-start.5 = (bf16[4,272,128]{2,1,0:T(8,128)(2,1)}, bf16[4,272,128]{2,1,0:T(8,128)(2,1)S(1)}, u32[]{:S(2)}) copy-start(bf16[4,272,128]{2,1,0:T(8,128)(2,1)S(1)} %collective-permute-done.5.refs_6_) | copy-start | bytes 835588
  111.2 8.5 %collective-permute-start.7 = (bf16[272,128]{1,0:T(8,128)(2,1)}, bf16[272,128]{1,0:T(8,128)(2,1)S(1)}, u32[]{:S(2)}, u32[]{:S(2)}) collective-permute-start(bf16[272,128]{1,0:T(8,128)(2,1)} %get-tuple-element.40), channel_id=1, source_target_pairs={{0,4},{1,5},{2,6},{3,7},{4,8},{5,9},{6,10},{7,11},{8,12},{9,13},{1... | collective-permute-start | bytes 208904 | tf_op jit(solution)/shard_map/ppermute | solution.py:195
  112.3 11.2 %collective-permute-start.8 = (bf16[272,128]{1,0:T(8,128)(2,1)}, bf16[272,128]{1,0:T(8,128)(2,1)S(1)}, u32[]{:S(2)}, u32[]{:S(2)}) collective-permute-start(bf16[272,128]{1,0:T(8,128)(2,1)} %get-tuple-element.41), channel_id=1, source_target_pairs={{0,8},{1,9},{2,10},{3,11},{4,12},{5,13},{6,14},{7,15},{8,0},{9,1},... | collective-permute-start | bytes 208904 | tf_op jit(solution)/shard_map/ppermute | solution.py:195
  115.6 9.4 %collective-permute-start.9 = (bf16[272,128]{1,0:T(8,128)(2,1)}, bf16[272,128]{1,0:T(8,128)(2,1)S(1)}, u32[]{:S(2)}, u32[]{:S(2)}) collective-permute-start(bf16[272,128]{1,0:T(8,128)(2,1)} %get-tuple-element.42), channel_id=1, source_target_pairs={{0,12},{1,13},{2,14},{3,15},{4,0},{5,1},{6,2},{7,3},{8,4},{9,5},{1... | collective-permute-start | bytes 208904 | tf_op jit(solution)/shard_map/ppermute | solution.py:195
  116.7 8.3 %collective-permute-start.10 = (bf16[272,128]{1,0:T(8,128)(2,1)}, bf16[272,128]{1,0:T(8,128)(2,1)S(1)}, u32[]{:S(2)}, u32[]{:S(2)}) collective-permute-start(bf16[272,128]{1,0:T(8,128)(2,1)} %get-tuple-element.44), channel_id=1, source_target_pairs={{0,1},{1,2},{2,3},{3,0},{4,5},{5,6},{6,7},{7,4},{8,9},{9,10},{10,1... | collective-permute-start | bytes 208904 | tf_op jit(solution)/shard_map/ppermute | solution.py:195
  119.7 8.4 %copy-start.6 = (bf16[272,128]{1,0:T(8,128)(2,1)}, bf16[272,128]{1,0:T(8,128)(2,1)S(1)}, u32[]{:S(2)}) copy-start(bf16[272,128]{1,0:T(8,128)(2,1)S(1)} %collective-permute-done.7.refs_1_) | copy-start | bytes 208900
  119.7 6.3 %collective-permute-start.11 = (bf16[272,128]{1,0:T(8,128)(2,1)}, bf16[272,128]{1,0:T(8,128)(2,1)S(1)}, u32[]{:S(2)}, u32[]{:S(2)}) collective-permute-start(bf16[272,128]{1,0:T(8,128)(2,1)} %get-tuple-element.45), channel_id=1, source_target_pairs={{0,2},{1,3},{2,0},{3,1},{4,6},{5,7},{6,4},{7,5},{8,10},{9,11},{10,... | collective-permute-start | bytes 208904 | tf_op jit(solution)/shard_map/ppermute | solution.py:195
  123.5 4.5 %copy-start.7 = (bf16[272,128]{1,0:T(8,128)(2,1)}, bf16[272,128]{1,0:T(8,128)(2,1)S(1)}, u32[]{:S(2)}) copy-start(bf16[272,128]{1,0:T(8,128)(2,1)S(1)} %collective-permute-done.8.refs_2_) | copy-start | bytes 208900
  123.5 4.5 %collective-permute-start.12 = (bf16[272,128]{1,0:T(8,128)(2,1)}, bf16[272,128]{1,0:T(8,128)(2,1)S(1)}, u32[]{:S(2)}, u32[]{:S(2)}) collective-permute-start(bf16[272,128]{1,0:T(8,128)(2,1)} %get-tuple-element.46), channel_id=1, source_target_pairs={{0,3},{1,0},{2,1},{3,2},{4,7},{5,4},{6,5},{7,6},{8,11},{9,8},{10,9... | collective-permute-start | bytes 208904 | tf_op jit(solution)/shard_map/ppermute | solution.py:195
  125.0 3.1 %copy-start.8 = (bf16[272,128]{1,0:T(8,128)(2,1)}, bf16[272,128]{1,0:T(8,128)(2,1)S(1)}, u32[]{:S(2)}) copy-start(bf16[272,128]{1,0:T(8,128)(2,1)S(1)} %collective-permute-done.9.refs_3_) | copy-start | bytes 208900
  125.0 3.1 %copy-start.9 = (bf16[272,128]{1,0:T(8,128)(2,1)}, bf16[272,128]{1,0:T(8,128)(2,1)S(1)}, u32[]{:S(2)}) copy-start(bf16[272,128]{1,0:T(8,128)(2,1)S(1)} %collective-permute-done.10.refs_5_) | copy-start | bytes 208900
  126.0 2.1 copy-start.10
  128.0 0.6 copy-start.11
  158.8 1.3 copy-start

commit v4 on v3

--- a/solution.py
+++ b/solution.py
@@ -228,20 +228,20 @@
         both = jnp.where(lane2 > row2, upper, upper.T)
         state_ref[m] = jnp.where(lane2 == row2, diag[m] + 0.1, both)
 
-    lane8, sub8 = iota2((8, size), 1), iota2((8, size), 0)
-    for r0 in range(0, size, 8):
-        panel = state_ref[:, r0 : r0 + 8, :]
-        for k in range(8):
+    deep = 16
+    lanes, subs = iota2((deep, size), 1), iota2((deep, size), 0)
+    for r0 in range(0, size, deep):
+        panel = state_ref[:, r0 : r0 + deep, :]
+        for k in range(deep):
             c = r0 + k
             col = panel[:, :, c : c + 1]
             pivot = panel[:, k : k + 1, c : c + 1]
             rk = lax.rsqrt(pivot)
-            rk = rk * (1.5 - 0.5 * pivot * rk * rk)
-            lead = jnp.where(lane8[:1] == c, rk, panel[:, k : k + 1, :] * rk)
-            kept = jnp.where(lane8 == c, 0.0, panel) - (col * rk) * lead
-            panel = jnp.where(sub8 > k, kept, jnp.where(sub8 == k, lead, panel))
-        rest = r0 + 8
-        panel = jnp.where((lane8 < rest) & (lane8 > r0 + sub8), 0.0, panel)
+            lead = jnp.where(lanes[:1] == c, rk, panel[:, k : k + 1, :] * rk)
+            kept = jnp.where(lanes == c, 0.0, panel) - (col * rk) * lead
+            panel = jnp.where(subs > k, kept, jnp.where(subs == k, lead, panel))
+        rest = r0 + deep
+        panel = jnp.where((lanes < rest) & (lanes > r0 + subs), 0.0, panel)
         state_ref[:, r0:rest, :] = panel
         if rest < size:
             h, m_, l = split3(panel)
@@ -313,8 +313,8 @@
             return
         env = jnp.swapaxes(e_buf[i], 0, 1)
         for u in range(channels):
-            alone = eye if u == 0 else jnp.zeros_like(eye)
-            wide_buf[i, :, u * size : (u + 1) * size] = jnp.where(first, alone, env[u])
+            block = jnp.where(first, eye, env[u]) if u == 0 else env[u]
+            wide_buf[i, :, u * size : (u + 1) * size] = block
         saves.append(copy(wide_buf.at[i], wide_ref.at[i], sems.at[3, i]))
         saves[-1].start()
 

time: 228 us -> 225 us (0.987)
  Pallas kernels: 57.3 us -> 53.9 us
    pallas_call x1, Pallas kernels: 17.1 us -> 14.7 us  [inverse_factors(): pl.pallas_call(functools.partial(factor_kernel, total_rows=total_rows), o...]
  transfers between devices with their start and end apart: 14 -> 14, of which waited for: 5 -> 5; matrix products, arithmetic and copies ran while one was open for 0% -> 0% of each run, Pallas kernels for 19% -> 18%
where the time goes in v4:
time: 225 us
  blocking collectives  91.1 us (40%)
  Pallas kernels  53.9 us (24%)
  waiting for transfers between devices  45 us (20%)
  starting transfers between devices  31.5 us (14%)
    all_to_all x2, blocking collectives, exchange(): return lax.all_to_all(value, 'sec', split_axis=0, concat_axis=0, tiled=True)  91.1 us
    ppermute x12, waiting for transfers between devices, turned_round(): moved.append(lax.ppermute(parts[along], 'sec', pairs))  45 us
    ppermute x12, starting transfers between devices, turned_round(): moved.append(lax.ppermute(parts[along], 'sec', pairs))  25.9 us
    pallas_call x2, Pallas kernels, matvec(): pl.pallas_call(functools.partial(matvec_kernel, part=part, group=group),...  21.9 us
    pallas_call x1, Pallas kernels, inverse_factors(): pl.pallas_call(functools.partial(factor_kernel, total_rows=total_rows), o...  14.7 us
    pallas_call x1, Pallas kernels, front(): pl.pallas_call(functools.partial(front_kernel, width=width, parts=parts),...  11.7 us
  transfers between devices with their start and end apart: 14, of which 5 were waited for; matrix products, arithmetic and copies ran while one was open for 0% of the time, Pallas kernels for 18%

profile of v4, /device:TPU:32, one launch (start us, length us, event | category | flops | bytes accessed | tf_op | source)
XLA Modules:
  0.0 224.5 jit_solution(4284420533150789364)
XLA Ops:
  0.0 1.9 collective-permute-start
  1.9 0.7 pad_add_fusion.where_ref
  2.6 11.7 %front.1 = (s32[32]{0:T(128)}, bf16[16,128,512]{2,1,0:T(8,128)(2,1)}, bf16[16,128,512]{2,1,0:T(8,128)(2,1)}, bf16[4,272,128]{2,1,0:T(8,128)(2,1)}, bf16[4,272,12...) custom-call(s32[2]{0:T(128)} %pad_add_fusion.where_ref, ...), custom_call_target="tpu_custom_call" | custom-call | tf_op jit(solution)/shard_map/front/pallas_call | solution.py:128
  14.3 0.0 copy-start.12
  14.3 36.4 %all_to_all.15.v_ref = bf16[16,128,512]{2,1,0:T(8,128)(2,1)} all-to-all(bf16[16,128,512]{2,1,0:T(8,128)(2,1)} %get-tuple-element.30), channel_id=1, replica_groups=mesh['seg'=8,'sec'=16] {'sec'}, dimensions={0} | all-to-all | bytes 4194304 | tf_op jit(solution)/shard_map/all_to_all | solution.py:421
  50.7 3.7 %all-to-all-start = ((bf16[16,128,512]{2,1,0:T(8,128)(2,1)}), bf16[16,128,512]{2,1,0:T(8,128)(2,1)S(1)}, u32[]{:S(2)}, u32[]{:S(2)}) async-start(bf16[16,128,512]{2,1,0:T(8,128)(2,1)} %get-tuple-element.29), calls=%async_computation | async-start | bytes 4194304 | tf_op jit(solution)/shard_map/all_to_all | solution.py:421
  54.4 0.0 copy-done.12
  54.4 1.9 collective-permute-start.1
  56.3 2.7 %collective-permute-start.2 = (bf16[4,272,128]{2,1,0:T(8,128)(2,1)}, bf16[4,272,128]{2,1,0:T(8,128)(2,1)S(1)}, u32[]{:S(2)}, u32[]{:S(2)}) collective-permute-start(bf16[4,272,128]{2,1,0:T(8,128)(2,1)} %get-tuple-element.33), channel_id=1, source_target_pairs={{0,2},{1,3},{2,0},{3,1},{4,6},{5,7},{6,4},{7,5},{8,10},{9,11},{10,... | collective-permute-start | bytes 835592 | tf_op jit(solution)/shard_map/ppermute | solution.py:195
  59.0 1.5 collective-permute-start.3
  60.5 1.5 collective-permute-start.4
  62.0 27.8 %collective-permute-done.1.refs_1_ = bf16[4,272,128]{2,1,0:T(8,128)(2,1)S(1)} collective-permute-done((bf16[4,272,128]{2,1,0:T(8,128)(2,1)S(1)}, bf16[4,272,128]{2,1,0:T(8,128)(2,1)S(1)}, u32[]{:S(2)}, u32[]{:S(2)}) %collective-permute-start.1) | collective-permute-done | bytes 278560 | tf_op jit(solution)/shard_map/ppermute | solution.py:195
  89.7 2.9 %collective-permute-start.5 = (bf16[4,272,128]{2,1,0:T(8,128)(2,1)}, bf16[4,272,128]{2,1,0:T(8,128)(2,1)S(1)}, u32[]{:S(2)}, u32[]{:S(2)}) collective-permute-start(bf16[4,272,128]{2,1,0:T(8,128)(2,1)} %get-tuple-element.37), channel_id=1, source_target_pairs={{0,8},{1,9},{2,10},{3,11},{4,12},{5,13},{6,14},{7,15},{8,0},{9,1},... | collective-permute-start | bytes 835592 | tf_op jit(solution)/shard_map/ppermute | solution.py:195
  92.6 7.4 %collective-permute-done.2.refs_2_ = bf16[4,272,128]{2,1,0:T(8,128)(2,1)S(1)} collective-permute-done((bf16[4,272,128]{2,1,0:T(8,128)(2,1)}, bf16[4,272,128]{2,1,0:T(8,128)(2,1)S(1)}, u32[]{:S(2)}, u32[]{:S(2)}) %collective-permute-start.2) | collective-permute-done | bytes 278560 | tf_op jit(solution)/shard_map/ppermute | solution.py:195
  100.0 1.7 collective-permute-start.6
  101.7 0.0 collective-permute-done.3.refs_3_
  101.7 0.0 collective-permute-done.4.refs_5_
  101.7 0.0 copy-start.4
  101.7 0.0 collective-permute-done.5.refs_6_
  101.7 0.0 copy-start.5
  101.8 6.8 %collective-permute-done.6.refs_7_ = bf16[4,272,128]{2,1,0:T(8,128)(2,1)} collective-permute-done((bf16[4,272,128]{2,1,0:T(8,128)(2,1)}, bf16[4,272,128]{2,1,0:T(8,128)(2,1)}, u32[]{:S(2)}, u32[]{:S(2)}) %collective-permute-start.6) | collective-permute-done | bytes 278560 | tf_op jit(solution)/shard_map/ppermute | solution.py:195
  108.6 0.0 copy-done.1
  108.6 0.0 copy-done.2
  108.6 0.0 copy-done.3
  108.6 0.0 copy-done.4
  108.6 2.5 %sums.1 = (bf16[272,128]{1,0:T(8,128)(2,1)}, bf16[272,128]{1,0:T(8,128)(2,1)}, bf16[272,128]{1,0:T(8,128)(2,1)}, bf16[272,128]{1,0:T(8,128)(2,1)}, bf16[272,128]...) custom-call(s32[32]{0:T(128)} %get-tuple-element.28.table_ref, ...), custom_call_target="tpu_custom_call" | custom-call | tf_op jit(solution)/shard_map/sums/pallas_call | solution.py:177
  111.2 1.1 collective-permute-start.7
  112.3 3.3 %collective-permute-start.8 = (bf16[272,128]{1,0:T(8,128)(2,1)}, bf16[272,128]{1,0:T(8,128)(2,1)S(1)}, u32[]{:S(2)}, u32[]{:S(2)}) collective-permute-start(bf16[272,128]{1,0:T(8,128)(2,1)} %get-tuple-element.41), channel_id=1, source_target_pairs={{0,8},{1,9},{2,10},{3,11},{4,12},{5,13},{6,14},{7,15},{8,0},{9,1},... | collective-permute-start | bytes 208904 | tf_op jit(solution)/shard_map/ppermute | solution.py:195
  115.6 1.1 collective-permute-start.9
  116.7 3.0 %collective-permute-start.10 = (bf16[272,128]{1,0:T(8,128)(2,1)}, bf16[272,128]{1,0:T(8,128)(2,1)S(1)}, u32[]{:S(2)}, u32[]{:S(2)}) collective-permute-start(bf16[272,128]{1,0:T(8,128)(2,1)} %get-tuple-element.44), channel_id=1, source_target_pairs={{0,1},{1,2},{2,3},{3,0},{4,5},{5,6},{6,7},{7,4},{8,9},{9,10},{10,1... | collective-permute-start | bytes 208904 | tf_op jit(solution)/shard_map/ppermute | solution.py:195
  119.7 0.0 collective-permute-done.7.refs_1_
  119.7 3.8 %collective-permute-start.11 = (bf16[272,128]{1,0:T(8,128)(2,1)}, bf16[272,128]{1,0:T(8,128)(2,1)S(1)}, u32[]{:S(2)}, u32[]{:S(2)}) collective-permute-start(bf16[272,128]{1,0:T(8,128)(2,1)} %get-tuple-element.45), channel_id=1, source_target_pairs={{0,2},{1,3},{2,0},{3,1},{4,6},{5,7},{6,4},{7,5},{8,10},{9,11},{10,... | collective-permute-start | bytes 208904 | tf_op jit(solution)/shard_map/ppermute | solution.py:195
  123.5 0.0 collective-permute-done.8.refs_2_
  123.5 1.5 collective-permute-start.12
  125.0 0.0 collective-permute-done.9.refs_3_
  125.0 0.0 collective-permute-done.10.refs_5_
  125.0 1.0 collective-permute-done.11.refs_6_
  126.0 2.0 collective-permute-done.12.refs_7_
  128.1 0.6 copy-done.11
  128.7 14.7 %factor.1 = (bf16[8,128,256]{2,1,0:T(8,128)(2,1)}, bf16[8,128,384]{2,1,0:T(8,128)(2,1)}) custom-call(s32[32]{0:T(128)} %get-tuple-element.28.table_ref, bf16[272,128]{1,0:T(8,128)(2,1)} %get-tuple-element.39.refs_0_, bf16[272,128]{1,0:T(8,128)(2,1)} %copy-done.6, bf16[272,128]{1,0:T(8,128)(2,1)} %copy-done.7, bf16[272,128]{1,0:T(8,128)(2,1)} %copy-done.8, ...), custom_call_target="tpu_custom_call" | custom-call | tf_op jit(solution)/shard_map/factor/pallas_call | solution.py:272
  143.4 0.0 collective-permute-done.e_ref
  143.4 12.0 %shard_map.73 = (bf16[16,128,1024]{2,1,0:T(8,128)(2,1)}, bf16[8,128,3072]{2,1,0:T(8,128)(2,1)}) custom-call(s32[32]{0:T(128)} %get-tuple-element.28.table_ref, bf16[16,128,512]{2,1,0:T(8,128)(2,1)} %all_to_all.15.v_ref, bf16[8,128,24,128]{3,2,1,0:T(8,128)(2,1)} %collective-permute-done.e_ref, f32[24,1024]{1,0:T(8,128)} %bitcast.9, ...), custom_call_target="tpu_custom_call" | custom-call | tf_op jit(solution)/shard_map/pallas_call | solution.py:377
  155.4 0.0 all-to-all-done.v_ref
  155.4 0.0 copy-start
  155.4 1.3 copy-done
  156.7 9.8 %shard_map.74 = bf16[16,128,1024]{2,1,0:T(8,128)(2,1)} custom-call(s32[32]{0:T(128)} %get-tuple-element.28.table_ref, bf16[16,128,512]{2,1,0:T(8,128)(2,1)} %copy-done, bf16[8,128,3072]{2,1,0:T(8,128)(2,1)} %get-tuple-element.49.e_ref, f32[24,1024]{1,0:T(8,128)} %bitcast.10, ...), custom_call_target="tpu_custom_call", output_to_operand_aliasing={{}: (6, {})} | custom-call | tf_op jit(solution)/shard_map/pallas_call | solution.py:377
  166.6 54.7 %all_to_all.16.x_ref = bf16[16,128,1024]{2,1,0:T(8,128)(2,1)} all-to-all(bf16[16,128,1024]{2,1,0:T(8,128)(2,1)} %shard_map.74), channel_id=1, replica_groups=mesh['seg'=8,'sec'=16] {'sec'}, dimensions={0} | all-to-all | bytes 8388608 | tf_op jit(solution)/shard_map/all_to_all | solution.py:421
  221.3 3.1 %gather.1 = bf16[8,128,1024]{2,1,0:T(8,128)(2,1)} custom-call(s32[32]{0:T(128)} %get-tuple-element.28.table_ref, bf16[16,128,1024]{2,1,0:T(8,128)(2,1)} %all_to_all.16.x_ref), custom_call_target="tpu_custom_call" | custom-call | tf_op jit(solution)/shard_map/gather/pallas_call | solution.py:410
  (15 shorter events, 0.0 us)
Async XLA Ops:
  0.0 143.4 %collective-permute-start = (bf16[8,128,24,128]{3,2,1,0:T(8,128)(2,1)}, bf16[8,128,24,128]{3,2,1,0:T(8,128)(2,1)}, u32[]{:S(2)}, u32[]{:S(2)}) collective-permute-start(bf16[8,128,24,128]{3,2,1,0:T(8,128)(2,1)} %bitcast.11), channel_id=1, source_target_pairs={{0,16},{16,32},{32,48},{48,64},{64,80},{80,96},{96,112},{1,17},{17... | collective-permute-start | bytes 18874376 | tf_op jit(solution)/shard_map/ppermute | solution.py:20
  14.3 40.2 %copy-start.12 = (bf16[4,272,128]{2,1,0:T(8,128)(2,1)S(1)}, bf16[4,272,128]{2,1,0:T(8,128)(2,1)}, u32[]{:S(2)}) copy-start(bf16[4,272,128]{2,1,0:T(8,128)(2,1)} %get-tuple-element.32) | copy-start | bytes 835588
  50.7 104.7 %all-to-all-start = ((bf16[16,128,512]{2,1,0:T(8,128)(2,1)}), bf16[16,128,512]{2,1,0:T(8,128)(2,1)S(1)}, u32[]{:S(2)}, u32[]{:S(2)}) async-start(bf16[16,128,512]{2,1,0:T(8,128)(2,1)} %get-tuple-element.29), calls=%async_computation | async-start | bytes 4194304 | tf_op jit(solution)/shard_map/all_to_all | solution.py:421
  54.4 35.3 %collective-permute-start.1 = (bf16[4,272,128]{2,1,0:T(8,128)(2,1)S(1)}, bf16[4,272,128]{2,1,0:T(8,128)(2,1)S(1)}, u32[]{:S(2)}, u32[]{:S(2)}) collective-permute-start(bf16[4,272,128]{2,1,0:T(8,128)(2,1)S(1)} %copy-done.12), channel_id=1, source_target_pairs={{0,1},{1,2},{2,3},{3,0},{4,5},{5,6},{6,7},{7,4},{8,9},{9,10},{10,1... | collective-permute-start | bytes 835592 | tf_op jit(solution)/shard_map/ppermute | solution.py:195
  56.3 43.7 %collective-permute-start.2 = (bf16[4,272,128]{2,1,0:T(8,128)(2,1)}, bf16[4,272,128]{2,1,0:T(8,128)(2,1)S(1)}, u32[]{:S(2)}, u32[]{:S(2)}) collective-permute-start(bf16[4,272,128]{2,1,0:T(8,128)(2,1)} %get-tuple-element.33), channel_id=1, source_target_pairs={{0,2},{1,3},{2,0},{3,1},{4,6},{5,7},{6,4},{7,5},{8,10},{9,11},{10,... | collective-permute-start | bytes 835592 | tf_op jit(solution)/shard_map/ppermute | solution.py:195
  59.0 42.7 %collective-permute-start.3 = (bf16[4,272,128]{2,1,0:T(8,128)(2,1)}, bf16[4,272,128]{2,1,0:T(8,128)(2,1)S(1)}, u32[]{:S(2)}, u32[]{:S(2)}) collective-permute-start(bf16[4,272,128]{2,1,0:T(8,128)(2,1)} %get-tuple-element.34), channel_id=1, source_target_pairs={{0,3},{1,0},{2,1},{3,2},{4,7},{5,4},{6,5},{7,6},{8,11},{9,8},{10,9... | collective-permute-start | bytes 835592 | tf_op jit(solution)/shard_map/ppermute | solution.py:195
  60.5 41.3 %collective-permute-start.4 = (bf16[4,272,128]{2,1,0:T(8,128)(2,1)}, bf16[4,272,128]{2,1,0:T(8,128)(2,1)S(1)}, u32[]{:S(2)}, u32[]{:S(2)}) collective-permute-start(bf16[4,272,128]{2,1,0:T(8,128)(2,1)} %get-tuple-element.36), channel_id=1, source_target_pairs={{0,4},{1,5},{2,6},{3,7},{4,8},{5,9},{6,10},{7,11},{8,12},{9,13},{1... | collective-permute-start | bytes 835592 | tf_op jit(solution)/shard_map/ppermute | solution.py:195
  89.7 18.9 %copy-start.1 = (bf16[4,272,128]{2,1,0:T(8,128)(2,1)}, bf16[4,272,128]{2,1,0:T(8,128)(2,1)S(1)}, u32[]{:S(2)}) copy-start(bf16[4,272,128]{2,1,0:T(8,128)(2,1)S(1)} %collective-permute-done.1.refs_1_) | copy-start | bytes 835588
  89.7 12.0 %collective-permute-start.5 = (bf16[4,272,128]{2,1,0:T(8,128)(2,1)}, bf16[4,272,128]{2,1,0:T(8,128)(2,1)S(1)}, u32[]{:S(2)}, u32[]{:S(2)}) collective-permute-start(bf16[4,272,128]{2,1,0:T(8,128)(2,1)} %get-tuple-element.37), channel_id=1, source_target_pairs={{0,8},{1,9},{2,10},{3,11},{4,12},{5,13},{6,14},{7,15},{8,0},{9,1},... | collective-permute-start | bytes 835592 | tf_op jit(solution)/shard_map/ppermute | solution.py:195
  100.0 8.6 %copy-start.2 = (bf16[4,272,128]{2,1,0:T(8,128)(2,1)}, bf16[4,272,128]{2,1,0:T(8,128)(2,1)S(1)}, u32[]{:S(2)}) copy-start(bf16[4,272,128]{2,1,0:T(8,128)(2,1)S(1)} %collective-permute-done.2.refs_2_) | copy-start | bytes 835588
  100.0 8.6 %collective-permute-start.6 = (bf16[4,272,128]{2,1,0:T(8,128)(2,1)}, bf16[4,272,128]{2,1,0:T(8,128)(2,1)}, u32[]{:S(2)}, u32[]{:S(2)}) collective-permute-start(bf16[4,272,128]{2,1,0:T(8,128)(2,1)} %get-tuple-element.38), channel_id=1, source_target_pairs={{0,12},{1,13},{2,14},{3,15},{4,0},{5,1},{6,2},{7,3},{8,4},{9,5},{1... | collective-permute-start | bytes 835592 | tf_op jit(solution)/shard_map/ppermute | solution.py:195
  101.7 6.9 %copy-start.3 = (bf16[4,272,128]{2,1,0:T(8,128)(2,1)}, bf16[4,272,128]{2,1,0:T(8,128)(2,1)S(1)}, u32[]{:S(2)}) copy-start(bf16[4,272,128]{2,1,0:T(8,128)(2,1)S(1)} %collective-permute-done.3.refs_3_) | copy-start | bytes 835588
  101.7 6.9 %copy-start.4 = (bf16[4,272,128]{2,1,0:T(8,128)(2,1)}, bf16[4,272,128]{2,1,0:T(8,128)(2,1)S(1)}, u32[]{:S(2)}) copy-start(bf16[4,272,128]{2,1,0:T(8,128)(2,1)S(1)} %collective-permute-done.4.refs_5_) | copy-start | bytes 835588
  101.7 6.9 %copy-start.5 = (bf16[4,272,128]{2,1,0:T(8,128)(2,1)}, bf16[4,272,128]{2,1,0:T(8,128)(2,1)S(1)}, u32[]{:S(2)}) copy-start(bf16[4,272,128]{2,1,0:T(8,128)(2,1)S(1)} %collective-permute-done.5.refs_6_) | copy-start | bytes 835588
  111.2 8.5 %collective-permute-start.7 = (bf16[272,128]{1,0:T(8,128)(2,1)}, bf16[272,128]{1,0:T(8,128)(2,1)S(1)}, u32[]{:S(2)}, u32[]{:S(2)}) collective-permute-start(bf16[272,128]{1,0:T(8,128)(2,1)} %get-tuple-element.40), channel_id=1, source_target_pairs={{0,4},{1,5},{2,6},{3,7},{4,8},{5,9},{6,10},{7,11},{8,12},{9,13},{1... | collective-permute-start | bytes 208904 | tf_op jit(solution)/shard_map/ppermute | solution.py:195
  112.3 11.2 %collective-permute-start.8 = (bf16[272,128]{1,0:T(8,128)(2,1)}, bf16[272,128]{1,0:T(8,128)(2,1)S(1)}, u32[]{:S(2)}, u32[]{:S(2)}) collective-permute-start(bf16[272,128]{1,0:T(8,128)(2,1)} %get-tuple-element.41), channel_id=1, source_target_pairs={{0,8},{1,9},{2,10},{3,11},{4,12},{5,13},{6,14},{7,15},{8,0},{9,1},... | collective-permute-start | bytes 208904 | tf_op jit(solution)/shard_map/ppermute | solution.py:195
  115.6 9.4 %collective-permute-start.9 = (bf16[272,128]{1,0:T(8,128)(2,1)}, bf16[272,128]{1,0:T(8,128)(2,1)S(1)}, u32[]{:S(2)}, u32[]{:S(2)}) collective-permute-start(bf16[272,128]{1,0:T(8,128)(2,1)} %get-tuple-element.42), channel_id=1, source_target_pairs={{0,12},{1,13},{2,14},{3,15},{4,0},{5,1},{6,2},{7,3},{8,4},{9,5},{1... | collective-permute-start | bytes 208904 | tf_op jit(solution)/shard_map/ppermute | solution.py:195
  116.7 8.3 %collective-permute-start.10 = (bf16[272,128]{1,0:T(8,128)(2,1)}, bf16[272,128]{1,0:T(8,128)(2,1)S(1)}, u32[]{:S(2)}, u32[]{:S(2)}) collective-permute-start(bf16[272,128]{1,0:T(8,128)(2,1)} %get-tuple-element.44), channel_id=1, source_target_pairs={{0,1},{1,2},{2,3},{3,0},{4,5},{5,6},{6,7},{7,4},{8,9},{9,10},{10,1... | collective-permute-start | bytes 208904 | tf_op jit(solution)/shard_map/ppermute | solution.py:195
  119.7 8.4 %copy-start.6 = (bf16[272,128]{1,0:T(8,128)(2,1)}, bf16[272,128]{1,0:T(8,128)(2,1)S(1)}, u32[]{:S(2)}) copy-start(bf16[272,128]{1,0:T(8,128)(2,1)S(1)} %collective-permute-done.7.refs_1_) | copy-start | bytes 208900
  119.7 6.3 %collective-permute-start.11 = (bf16[272,128]{1,0:T(8,128)(2,1)}, bf16[272,128]{1,0:T(8,128)(2,1)S(1)}, u32[]{:S(2)}, u32[]{:S(2)}) collective-permute-start(bf16[272,128]{1,0:T(8,128)(2,1)} %get-tuple-element.45), channel_id=1, source_target_pairs={{0,2},{1,3},{2,0},{3,1},{4,6},{5,7},{6,4},{7,5},{8,10},{9,11},{10,... | collective-permute-start | bytes 208904 | tf_op jit(solution)/shard_map/ppermute | solution.py:195
  123.5 4.5 %copy-start.7 = (bf16[272,128]{1,0:T(8,128)(2,1)}, bf16[272,128]{1,0:T(8,128)(2,1)S(1)}, u32[]{:S(2)}) copy-start(bf16[272,128]{1,0:T(8,128)(2,1)S(1)} %collective-permute-done.8.refs_2_) | copy-start | bytes 208900
  123.5 4.5 %collective-permute-start.12 = (bf16[272,128]{1,0:T(8,128)(2,1)}, bf16[272,128]{1,0:T(8,128)(2,1)S(1)}, u32[]{:S(2)}, u32[]{:S(2)}) collective-permute-start(bf16[272,128]{1,0:T(8,128)(2,1)} %get-tuple-element.46), channel_id=1, source_target_pairs={{0,3},{1,0},{2,1},{3,2},{4,7},{5,4},{6,5},{7,6},{8,11},{9,8},{10,9... | collective-permute-start | bytes 208904 | tf_op jit(solution)/shard_map/ppermute | solution.py:195
  125.0 3.1 %copy-start.8 = (bf16[272,128]{1,0:T(8,128)(2,1)}, bf16[272,128]{1,0:T(8,128)(2,1)S(1)}, u32[]{:S(2)}) copy-start(bf16[272,128]{1,0:T(8,128)(2,1)S(1)} %collective-permute-done.9.refs_3_) | copy-start | bytes 208900
  125.0 3.1 %copy-start.9 = (bf16[272,128]{1,0:T(8,128)(2,1)}, bf16[272,128]{1,0:T(8,128)(2,1)S(1)}, u32[]{:S(2)}) copy-start(bf16[272,128]{1,0:T(8,128)(2,1)S(1)} %collective-permute-done.10.refs_5_) | copy-start | bytes 208900
  126.0 2.1 copy-start.10
  128.0 0.6 copy-start.11
  155.4 1.3 copy-start

commit v5 on v4

--- a/solution.py
+++ b/solution.py
@@ -30,7 +30,7 @@
 
 
 def front_kernel(
-    where_ref, before_ref, after_ref, kept_ref, vec_ref, x_ref, table_ref, *rest, width, parts
+    sec_ref, seg_ref, before_ref, after_ref, kept_ref, vec_ref, x_ref, table_ref, *rest, width, parts
 ):
     packs, outs = rest[:parts], rest[parts : parts + 2 * SIDE]
     place_ref, inv_ref, vec_buf, o_ref, diag_ref, load_sem, pack_sems, sems = rest[parts + 2 * SIDE :]
@@ -40,8 +40,8 @@
     half = size // 2
     each = width // 2
     cols = vec_buf.shape[2] // parts
-    base = where_ref[0] * width
-    mine_y, mine_x = where_ref[0] // SIDE, where_ref[0] % SIDE
+    base = sec_ref[0] * width
+    mine_y, mine_x = sec_ref[0] // SIDE, sec_ref[0] % SIDE
     load = pltpu.make_async_copy(vec_ref, vec_buf, load_sem)
 
     def pack(j, h):
@@ -61,13 +61,13 @@
             inv_ref[after_ref[i]] = i
             return carry
 
-        lax.fori_loop(0, before_ref.shape[0], invert, 0)
+        lax.fori_loop(0, before_ref.shape[0], invert, 0, unroll=8)
         for j in range(width):
             sector = before_ref[base + j]
             table_ref[j] = inv_ref[sector] // width
             table_ref[width + j] = place_ref[after_ref[base + j]] // width
             table_ref[2 * width + j] = kept_ref[sector]
-            table_ref[3 * width + j] = where_ref[j % 2]
+            table_ref[3 * width + j] = seg_ref[0] if j % 2 else sec_ref[0]
 
     @pl.when(step == 1)
     def _():
@@ -119,7 +119,7 @@
     return jnp.concatenate([high, exact - high], axis=0).astype(BF16)
 
 
-def front(where, before, after, kept, vectors, rows, parts, count=32):
+def front(sec, seg, before, after, kept, vectors, rows, parts, count=32):
     length, sectors, size = rows.shape
     width, _, cols = vectors.shape
     devices = sectors // width
@@ -131,7 +131,7 @@
         + [jax.ShapeDtypeStruct((devices, size, cols // parts), BF16)] * parts
         + [jax.ShapeDtypeStruct((SIDE, deep, size), BF16)] * (2 * SIDE),
         grid_spec=pltpu.PrefetchScalarGridSpec(
-            num_scalar_prefetch=4,
+            num_scalar_prefetch=5,
             grid=(sectors // count,),
             in_specs=[hbm, pl.BlockSpec((length, count, size), lambda i, *_: (0, i, 0))],
             out_specs=[pl.BlockSpec(memory_space=pltpu.SMEM)] + [hbm] * (parts + 2 * SIDE),
@@ -147,7 +147,7 @@
             ],
         ),
         name="front",
-    )(where, before, after, kept, vectors, rows)
+    )(sec, seg, before, after, kept, vectors, rows)
     return table, outs[:parts], outs[parts : parts + SIDE], outs[parts + SIDE :]
 
 
@@ -427,9 +427,9 @@
     width = left_envs.shape[1]
     total_rows = wave_block.shape[1] * lax.axis_size("sec")
     env = passed_along(left_envs[0], "seg", 1)
-    where = jnp.stack([lax.axis_index("sec"), lax.axis_index("seg")]).astype(jnp.int32)
+    sec, seg = [lax.axis_index(a).astype(jnp.int32).reshape(1) for a in ("sec", "seg")]
     table, packs, first, second = front(
-        where, slots_before, slots_after, kept_counts, next_vectors[0], wave_block[0], PARTS
+        sec, seg, slots_before, slots_after, kept_counts, next_vectors[0], wave_block[0], PARTS
     )
     arrived = []
     for h in range(PARTS):

time: 225 us -> 224 us (level)
  no operation moved by 1% of the time
where the time goes in v5:
time: 224 us; the launch traced here: 223 us
  blocking collectives  91.1 us (41%)
  Pallas kernels  53.4 us (24%)
  waiting for transfers between devices  45.1 us (20%)
  starting transfers between devices  31.5 us (14%)
    all_to_all x2, blocking collectives, exchange(): return lax.all_to_all(value, 'sec', split_axis=0, concat_axis=0, tiled=True)  91.1 us
    ppermute x12, waiting for transfers between devices, turned_round(): moved.append(lax.ppermute(parts[along], 'sec', pairs))  45.1 us
    ppermute x12, starting transfers between devices, turned_round(): moved.append(lax.ppermute(parts[along], 'sec', pairs))  25.9 us
    pallas_call x2, Pallas kernels, matvec(): pl.pallas_call(functools.partial(matvec_kernel, part=part, group=group),...  21.9 us
    pallas_call x1, Pallas kernels, inverse_factors(): pl.pallas_call(functools.partial(factor_kernel, total_rows=total_rows), o...  14.7 us
    pallas_call x1, Pallas kernels, front(): pl.pallas_call(functools.partial(front_kernel, width=width, parts=parts),...  11.2 us
  transfers between devices with their start and end apart: 14, of which 5 were waited for; matrix products, arithmetic and copies ran while one was open for 0% of the time, Pallas kernels for 18%

profile of v5, /device:TPU:32, one launch (start us, length us, event | category | flops | bytes accessed | tf_op | source)
XLA Modules:
  0.0 223.4 jit_solution(17043292542577175577)
XLA Ops:
  0.0 1.9 collective-permute-start
  1.9 11.2 %front.1 = (s32[32]{0:T(128)}, bf16[16,128,512]{2,1,0:T(8,128)(2,1)}, bf16[16,128,512]{2,1,0:T(8,128)(2,1)}, bf16[4,272,128]{2,1,0:T(8,128)(2,1)}, bf16[4,272,12...) custom-call(s32[1]{0:T(128)} %bitcast.sec_ref, ...), custom_call_target="tpu_custom_call" | custom-call | tf_op jit(solution)/shard_map/front/pallas_call | solution.py:128
  13.1 0.0 copy-start.12
  13.1 36.4 %all_to_all.15.v_ref = bf16[16,128,512]{2,1,0:T(8,128)(2,1)} all-to-all(bf16[16,128,512]{2,1,0:T(8,128)(2,1)} %get-tuple-element.30), channel_id=1, replica_groups=mesh['seg'=8,'sec'=16] {'sec'}, dimensions={0} | all-to-all | bytes 4194304 | tf_op jit(solution)/shard_map/all_to_all | solution.py:421
  49.6 3.7 %all-to-all-start = ((bf16[16,128,512]{2,1,0:T(8,128)(2,1)}), bf16[16,128,512]{2,1,0:T(8,128)(2,1)S(1)}, u32[]{:S(2)}, u32[]{:S(2)}) async-start(bf16[16,128,512]{2,1,0:T(8,128)(2,1)} %get-tuple-element.29), calls=%async_computation | async-start | bytes 4194304 | tf_op jit(solution)/shard_map/all_to_all | solution.py:421
  53.3 0.0 copy-done.12
  53.3 1.9 collective-permute-start.1
  55.2 2.7 %collective-permute-start.2 = (bf16[4,272,128]{2,1,0:T(8,128)(2,1)}, bf16[4,272,128]{2,1,0:T(8,128)(2,1)S(1)}, u32[]{:S(2)}, u32[]{:S(2)}) collective-permute-start(bf16[4,272,128]{2,1,0:T(8,128)(2,1)} %get-tuple-element.33), channel_id=1, source_target_pairs={{0,2},{1,3},{2,0},{3,1},{4,6},{5,7},{6,4},{7,5},{8,10},{9,11},{10,... | collective-permute-start | bytes 835592 | tf_op jit(solution)/shard_map/ppermute | solution.py:195
  57.9 1.5 collective-permute-start.3
  59.3 1.5 collective-permute-start.4
  60.8 27.8 %collective-permute-done.1.refs_1_ = bf16[4,272,128]{2,1,0:T(8,128)(2,1)S(1)} collective-permute-done((bf16[4,272,128]{2,1,0:T(8,128)(2,1)S(1)}, bf16[4,272,128]{2,1,0:T(8,128)(2,1)S(1)}, u32[]{:S(2)}, u32[]{:S(2)}) %collective-permute-start.1) | collective-permute-done | bytes 278560 | tf_op jit(solution)/shard_map/ppermute | solution.py:195
  88.6 2.9 %collective-permute-start.5 = (bf16[4,272,128]{2,1,0:T(8,128)(2,1)}, bf16[4,272,128]{2,1,0:T(8,128)(2,1)S(1)}, u32[]{:S(2)}, u32[]{:S(2)}) collective-permute-start(bf16[4,272,128]{2,1,0:T(8,128)(2,1)} %get-tuple-element.37), channel_id=1, source_target_pairs={{0,8},{1,9},{2,10},{3,11},{4,12},{5,13},{6,14},{7,15},{8,0},{9,1},... | collective-permute-start | bytes 835592 | tf_op jit(solution)/shard_map/ppermute | solution.py:195
  91.4 7.4 %collective-permute-done.2.refs_2_ = bf16[4,272,128]{2,1,0:T(8,128)(2,1)S(1)} collective-permute-done((bf16[4,272,128]{2,1,0:T(8,128)(2,1)}, bf16[4,272,128]{2,1,0:T(8,128)(2,1)S(1)}, u32[]{:S(2)}, u32[]{:S(2)}) %collective-permute-start.2) | collective-permute-done | bytes 278560 | tf_op jit(solution)/shard_map/ppermute | solution.py:195
  98.8 1.7 collective-permute-start.6
  100.6 0.0 collective-permute-done.3.refs_3_
  100.6 0.0 collective-permute-done.4.refs_5_
  100.6 0.0 copy-start.4
  100.6 0.0 collective-permute-done.5.refs_6_
  100.6 0.0 copy-start.5
  100.6 6.8 %collective-permute-done.6.refs_7_ = bf16[4,272,128]{2,1,0:T(8,128)(2,1)} collective-permute-done((bf16[4,272,128]{2,1,0:T(8,128)(2,1)}, bf16[4,272,128]{2,1,0:T(8,128)(2,1)}, u32[]{:S(2)}, u32[]{:S(2)}) %collective-permute-start.6) | collective-permute-done | bytes 278560 | tf_op jit(solution)/shard_map/ppermute | solution.py:195
  107.5 0.0 copy-done.1
  107.5 0.0 copy-done.3
  107.5 2.5 %sums.1 = (bf16[272,128]{1,0:T(8,128)(2,1)}, bf16[272,128]{1,0:T(8,128)(2,1)}, bf16[272,128]{1,0:T(8,128)(2,1)}, bf16[272,128]{1,0:T(8,128)(2,1)}, bf16[272,128]...) custom-call(s32[32]{0:T(128)} %get-tuple-element.28.table_ref, ...), custom_call_target="tpu_custom_call" | custom-call | tf_op jit(solution)/shard_map/sums/pallas_call | solution.py:177
  110.0 1.1 collective-permute-start.7
  111.1 3.3 %collective-permute-start.8 = (bf16[272,128]{1,0:T(8,128)(2,1)}, bf16[272,128]{1,0:T(8,128)(2,1)S(1)}, u32[]{:S(2)}, u32[]{:S(2)}) collective-permute-start(bf16[272,128]{1,0:T(8,128)(2,1)} %get-tuple-element.41), channel_id=1, source_target_pairs={{0,8},{1,9},{2,10},{3,11},{4,12},{5,13},{6,14},{7,15},{8,0},{9,1},... | collective-permute-start | bytes 208904 | tf_op jit(solution)/shard_map/ppermute | solution.py:195
  114.4 1.1 collective-permute-start.9
  115.5 3.0 %collective-permute-start.10 = (bf16[272,128]{1,0:T(8,128)(2,1)}, bf16[272,128]{1,0:T(8,128)(2,1)S(1)}, u32[]{:S(2)}, u32[]{:S(2)}) collective-permute-start(bf16[272,128]{1,0:T(8,128)(2,1)} %get-tuple-element.44), channel_id=1, source_target_pairs={{0,1},{1,2},{2,3},{3,0},{4,5},{5,6},{6,7},{7,4},{8,9},{9,10},{10,1... | collective-permute-start | bytes 208904 | tf_op jit(solution)/shard_map/ppermute | solution.py:195
  118.5 0.0 collective-permute-done.7.refs_1_
  118.5 3.8 %collective-permute-start.11 = (bf16[272,128]{1,0:T(8,128)(2,1)}, bf16[272,128]{1,0:T(8,128)(2,1)S(1)}, u32[]{:S(2)}, u32[]{:S(2)}) collective-permute-start(bf16[272,128]{1,0:T(8,128)(2,1)} %get-tuple-element.45), channel_id=1, source_target_pairs={{0,2},{1,3},{2,0},{3,1},{4,6},{5,7},{6,4},{7,5},{8,10},{9,11},{10,... | collective-permute-start | bytes 208904 | tf_op jit(solution)/shard_map/ppermute | solution.py:195
  122.4 0.0 collective-permute-done.8.refs_2_
  122.4 1.5 collective-permute-start.12
  123.8 0.0 collective-permute-done.9.refs_3_
  123.8 0.0 collective-permute-done.10.refs_5_
  123.8 1.0 collective-permute-done.11.refs_6_
  124.9 2.0 collective-permute-done.12.refs_7_
  126.9 0.0 copy-done.7
  126.9 0.0 copy-done.9
  126.9 0.0 copy-done.10
  126.9 0.6 copy-done.11
  127.5 14.7 %factor.1 = (bf16[8,128,256]{2,1,0:T(8,128)(2,1)}, bf16[8,128,384]{2,1,0:T(8,128)(2,1)}) custom-call(s32[32]{0:T(128)} %get-tuple-element.28.table_ref, bf16[272,128]{1,0:T(8,128)(2,1)} %get-tuple-element.39.refs_0_, bf16[272,128]{1,0:T(8,128)(2,1)} %copy-done.6, bf16[272,128]{1,0:T(8,128)(2,1)} %copy-done.7, bf16[272,128]{1,0:T(8,128)(2,1)} %copy-done.8, ...), custom_call_target="tpu_custom_call" | custom-call | tf_op jit(solution)/shard_map/factor/pallas_call | solution.py:272
  142.3 0.0 collective-permute-done.e_ref
  142.3 12.0 %shard_map.73 = (bf16[16,128,1024]{2,1,0:T(8,128)(2,1)}, bf16[8,128,3072]{2,1,0:T(8,128)(2,1)}) custom-call(s32[32]{0:T(128)} %get-tuple-element.28.table_ref, bf16[16,128,512]{2,1,0:T(8,128)(2,1)} %all_to_all.15.v_ref, bf16[8,128,24,128]{3,2,1,0:T(8,128)(2,1)} %collective-permute-done.e_ref, f32[24,1024]{1,0:T(8,128)} %bitcast.9, ...), custom_call_target="tpu_custom_call" | custom-call | tf_op jit(solution)/shard_map/pallas_call | solution.py:377
  154.3 0.0 all-to-all-done.v_ref
  154.3 0.0 copy-start
  154.3 1.3 copy-done
  155.6 9.9 %shard_map.74 = bf16[16,128,1024]{2,1,0:T(8,128)(2,1)} custom-call(s32[32]{0:T(128)} %get-tuple-element.28.table_ref, bf16[16,128,512]{2,1,0:T(8,128)(2,1)} %copy-done, bf16[8,128,3072]{2,1,0:T(8,128)(2,1)} %get-tuple-element.49.e_ref, f32[24,1024]{1,0:T(8,128)} %bitcast.10, ...), custom_call_target="tpu_custom_call", output_to_operand_aliasing={{}: (6, {})} | custom-call | tf_op jit(solution)/shard_map/pallas_call | solution.py:377
  165.5 54.7 %all_to_all.16.x_ref = bf16[16,128,1024]{2,1,0:T(8,128)(2,1)} all-to-all(bf16[16,128,1024]{2,1,0:T(8,128)(2,1)} %shard_map.74), channel_id=1, replica_groups=mesh['seg'=8,'sec'=16] {'sec'}, dimensions={0} | all-to-all | bytes 8388608 | tf_op jit(solution)/shard_map/all_to_all | solution.py:421
  220.1 3.1 %gather.1 = bf16[8,128,1024]{2,1,0:T(8,128)(2,1)} custom-call(s32[32]{0:T(128)} %get-tuple-element.28.table_ref, bf16[16,128,1024]{2,1,0:T(8,128)(2,1)} %all_to_all.16.x_ref), custom_call_target="tpu_custom_call" | custom-call | tf_op jit(solution)/shard_map/gather/pallas_call | solution.py:410
  (14 shorter events, 0.0 us)
Async XLA Ops:
  0.0 142.3 %collective-permute-start = (bf16[8,128,24,128]{3,2,1,0:T(8,128)(2,1)}, bf16[8,128,24,128]{3,2,1,0:T(8,128)(2,1)}, u32[]{:S(2)}, u32[]{:S(2)}) collective-permute-start(bf16[8,128,24,128]{3,2,1,0:T(8,128)(2,1)} %bitcast.11), channel_id=1, source_target_pairs={{0,16},{16,32},{32,48},{48,64},{64,80},{80,96},{96,112},{1,17},{17... | collective-permute-start | bytes 18874376 | tf_op jit(solution)/shard_map/ppermute | solution.py:20
  13.1 40.2 %copy-start.12 = (bf16[4,272,128]{2,1,0:T(8,128)(2,1)S(1)}, bf16[4,272,128]{2,1,0:T(8,128)(2,1)}, u32[]{:S(2)}) copy-start(bf16[4,272,128]{2,1,0:T(8,128)(2,1)} %get-tuple-element.32) | copy-start | bytes 835588
  49.6 104.7 %all-to-all-start = ((bf16[16,128,512]{2,1,0:T(8,128)(2,1)}), bf16[16,128,512]{2,1,0:T(8,128)(2,1)S(1)}, u32[]{:S(2)}, u32[]{:S(2)}) async-start(bf16[16,128,512]{2,1,0:T(8,128)(2,1)} %get-tuple-element.29), calls=%async_computation | async-start | bytes 4194304 | tf_op jit(solution)/shard_map/all_to_all | solution.py:421
  53.3 35.3 %collective-permute-start.1 = (bf16[4,272,128]{2,1,0:T(8,128)(2,1)S(1)}, bf16[4,272,128]{2,1,0:T(8,128)(2,1)S(1)}, u32[]{:S(2)}, u32[]{:S(2)}) collective-permute-start(bf16[4,272,128]{2,1,0:T(8,128)(2,1)S(1)} %copy-done.12), channel_id=1, source_target_pairs={{0,1},{1,2},{2,3},{3,0},{4,5},{5,6},{6,7},{7,4},{8,9},{9,10},{10,1... | collective-permute-start | bytes 835592 | tf_op jit(solution)/shard_map/ppermute | solution.py:195
  55.2 43.7 %collective-permute-start.2 = (bf16[4,272,128]{2,1,0:T(8,128)(2,1)}, bf16[4,272,128]{2,1,0:T(8,128)(2,1)S(1)}, u32[]{:S(2)}, u32[]{:S(2)}) collective-permute-start(bf16[4,272,128]{2,1,0:T(8,128)(2,1)} %get-tuple-element.33), channel_id=1, source_target_pairs={{0,2},{1,3},{2,0},{3,1},{4,6},{5,7},{6,4},{7,5},{8,10},{9,11},{10,... | collective-permute-start | bytes 835592 | tf_op jit(solution)/shard_map/ppermute | solution.py:195
  57.9 42.7 %collective-permute-start.3 = (bf16[4,272,128]{2,1,0:T(8,128)(2,1)}, bf16[4,272,128]{2,1,0:T(8,128)(2,1)S(1)}, u32[]{:S(2)}, u32[]{:S(2)}) collective-permute-start(bf16[4,272,128]{2,1,0:T(8,128)(2,1)} %get-tuple-element.34), channel_id=1, source_target_pairs={{0,3},{1,0},{2,1},{3,2},{4,7},{5,4},{6,5},{7,6},{8,11},{9,8},{10,9... | collective-permute-start | bytes 835592 | tf_op jit(solution)/shard_map/ppermute | solution.py:195
  59.3 41.3 %collective-permute-start.4 = (bf16[4,272,128]{2,1,0:T(8,128)(2,1)}, bf16[4,272,128]{2,1,0:T(8,128)(2,1)S(1)}, u32[]{:S(2)}, u32[]{:S(2)}) collective-permute-start(bf16[4,272,128]{2,1,0:T(8,128)(2,1)} %get-tuple-element.36), channel_id=1, source_target_pairs={{0,4},{1,5},{2,6},{3,7},{4,8},{5,9},{6,10},{7,11},{8,12},{9,13},{1... | collective-permute-start | bytes 835592 | tf_op jit(solution)/shard_map/ppermute | solution.py:195
  88.6 18.9 %copy-start.1 = (bf16[4,272,128]{2,1,0:T(8,128)(2,1)}, bf16[4,272,128]{2,1,0:T(8,128)(2,1)S(1)}, u32[]{:S(2)}) copy-start(bf16[4,272,128]{2,1,0:T(8,128)(2,1)S(1)} %collective-permute-done.1.refs_1_) | copy-start | bytes 835588
  88.6 12.0 %collective-permute-start.5 = (bf16[4,272,128]{2,1,0:T(8,128)(2,1)}, bf16[4,272,128]{2,1,0:T(8,128)(2,1)S(1)}, u32[]{:S(2)}, u32[]{:S(2)}) collective-permute-start(bf16[4,272,128]{2,1,0:T(8,128)(2,1)} %get-tuple-element.37), channel_id=1, source_target_pairs={{0,8},{1,9},{2,10},{3,11},{4,12},{5,13},{6,14},{7,15},{8,0},{9,1},... | collective-permute-start | bytes 835592 | tf_op jit(solution)/shard_map/ppermute | solution.py:195
  98.8 8.6 %copy-start.2 = (bf16[4,272,128]{2,1,0:T(8,128)(2,1)}, bf16[4,272,128]{2,1,0:T(8,128)(2,1)S(1)}, u32[]{:S(2)}) copy-start(bf16[4,272,128]{2,1,0:T(8,128)(2,1)S(1)} %collective-permute-done.2.refs_2_) | copy-start | bytes 835588
  98.8 8.6 %collective-permute-start.6 = (bf16[4,272,128]{2,1,0:T(8,128)(2,1)}, bf16[4,272,128]{2,1,0:T(8,128)(2,1)}, u32[]{:S(2)}, u32[]{:S(2)}) collective-permute-start(bf16[4,272,128]{2,1,0:T(8,128)(2,1)} %get-tuple-element.38), channel_id=1, source_target_pairs={{0,12},{1,13},{2,14},{3,15},{4,0},{5,1},{6,2},{7,3},{8,4},{9,5},{1... | collective-permute-start | bytes 835592 | tf_op jit(solution)/shard_map/ppermute | solution.py:195
  100.6 6.9 %copy-start.3 = (bf16[4,272,128]{2,1,0:T(8,128)(2,1)}, bf16[4,272,128]{2,1,0:T(8,128)(2,1)S(1)}, u32[]{:S(2)}) copy-start(bf16[4,272,128]{2,1,0:T(8,128)(2,1)S(1)} %collective-permute-done.3.refs_3_) | copy-start | bytes 835588
  100.6 6.9 %copy-start.4 = (bf16[4,272,128]{2,1,0:T(8,128)(2,1)}, bf16[4,272,128]{2,1,0:T(8,128)(2,1)S(1)}, u32[]{:S(2)}) copy-start(bf16[4,272,128]{2,1,0:T(8,128)(2,1)S(1)} %collective-permute-done.4.refs_5_) | copy-start | bytes 835588
  100.6 6.9 %copy-start.5 = (bf16[4,272,128]{2,1,0:T(8,128)(2,1)}, bf16[4,272,128]{2,1,0:T(8,128)(2,1)S(1)}, u32[]{:S(2)}) copy-start(bf16[4,272,128]{2,1,0:T(8,128)(2,1)S(1)} %collective-permute-done.5.refs_6_) | copy-start | bytes 835588
  110.0 8.5 %collective-permute-start.7 = (bf16[272,128]{1,0:T(8,128)(2,1)}, bf16[272,128]{1,0:T(8,128)(2,1)S(1)}, u32[]{:S(2)}, u32[]{:S(2)}) collective-permute-start(bf16[272,128]{1,0:T(8,128)(2,1)} %get-tuple-element.40), channel_id=1, source_target_pairs={{0,4},{1,5},{2,6},{3,7},{4,8},{5,9},{6,10},{7,11},{8,12},{9,13},{1... | collective-permute-start | bytes 208904 | tf_op jit(solution)/shard_map/ppermute | solution.py:195
  111.1 11.2 %collective-permute-start.8 = (bf16[272,128]{1,0:T(8,128)(2,1)}, bf16[272,128]{1,0:T(8,128)(2,1)S(1)}, u32[]{:S(2)}, u32[]{:S(2)}) collective-permute-start(bf16[272,128]{1,0:T(8,128)(2,1)} %get-tuple-element.41), channel_id=1, source_target_pairs={{0,8},{1,9},{2,10},{3,11},{4,12},{5,13},{6,14},{7,15},{8,0},{9,1},... | collective-permute-start | bytes 208904 | tf_op jit(solution)/shard_map/ppermute | solution.py:195
  114.4 9.4 %collective-permute-start.9 = (bf16[272,128]{1,0:T(8,128)(2,1)}, bf16[272,128]{1,0:T(8,128)(2,1)S(1)}, u32[]{:S(2)}, u32[]{:S(2)}) collective-permute-start(bf16[272,128]{1,0:T(8,128)(2,1)} %get-tuple-element.42), channel_id=1, source_target_pairs={{0,12},{1,13},{2,14},{3,15},{4,0},{5,1},{6,2},{7,3},{8,4},{9,5},{1... | collective-permute-start | bytes 208904 | tf_op jit(solution)/shard_map/ppermute | solution.py:195
  115.5 8.3 %collective-permute-start.10 = (bf16[272,128]{1,0:T(8,128)(2,1)}, bf16[272,128]{1,0:T(8,128)(2,1)S(1)}, u32[]{:S(2)}, u32[]{:S(2)}) collective-permute-start(bf16[272,128]{1,0:T(8,128)(2,1)} %get-tuple-element.44), channel_id=1, source_target_pairs={{0,1},{1,2},{2,3},{3,0},{4,5},{5,6},{6,7},{7,4},{8,9},{9,10},{10,1... | collective-permute-start | bytes 208904 | tf_op jit(solution)/shard_map/ppermute | solution.py:195
  118.5 8.4 %copy-start.6 = (bf16[272,128]{1,0:T(8,128)(2,1)}, bf16[272,128]{1,0:T(8,128)(2,1)S(1)}, u32[]{:S(2)}) copy-start(bf16[272,128]{1,0:T(8,128)(2,1)S(1)} %collective-permute-done.7.refs_1_) | copy-start | bytes 208900
  118.5 6.3 %collective-permute-start.11 = (bf16[272,128]{1,0:T(8,128)(2,1)}, bf16[272,128]{1,0:T(8,128)(2,1)S(1)}, u32[]{:S(2)}, u32[]{:S(2)}) collective-permute-start(bf16[272,128]{1,0:T(8,128)(2,1)} %get-tuple-element.45), channel_id=1, source_target_pairs={{0,2},{1,3},{2,0},{3,1},{4,6},{5,7},{6,4},{7,5},{8,10},{9,11},{10,... | collective-permute-start | bytes 208904 | tf_op jit(solution)/shard_map/ppermute | solution.py:195
  122.4 4.5 %copy-start.7 = (bf16[272,128]{1,0:T(8,128)(2,1)}, bf16[272,128]{1,0:T(8,128)(2,1)S(1)}, u32[]{:S(2)}) copy-start(bf16[272,128]{1,0:T(8,128)(2,1)S(1)} %collective-permute-done.8.refs_2_) | copy-start | bytes 208900
  122.4 4.5 %collective-permute-start.12 = (bf16[272,128]{1,0:T(8,128)(2,1)}, bf16[272,128]{1,0:T(8,128)(2,1)S(1)}, u32[]{:S(2)}, u32[]{:S(2)}) collective-permute-start(bf16[272,128]{1,0:T(8,128)(2,1)} %get-tuple-element.46), channel_id=1, source_target_pairs={{0,3},{1,0},{2,1},{3,2},{4,7},{5,4},{6,5},{7,6},{8,11},{9,8},{10,9... | collective-permute-start | bytes 208904 | tf_op jit(solution)/shard_map/ppermute | solution.py:195
  123.8 3.1 %copy-start.8 = (bf16[272,128]{1,0:T(8,128)(2,1)}, bf16[272,128]{1,0:T(8,128)(2,1)S(1)}, u32[]{:S(2)}) copy-start(bf16[272,128]{1,0:T(8,128)(2,1)S(1)} %collective-permute-done.9.refs_3_) | copy-start | bytes 208900
  123.8 3.1 %copy-start.9 = (bf16[272,128]{1,0:T(8,128)(2,1)}, bf16[272,128]{1,0:T(8,128)(2,1)S(1)}, u32[]{:S(2)}) copy-start(bf16[272,128]{1,0:T(8,128)(2,1)S(1)} %collective-permute-done.10.refs_5_) | copy-start | bytes 208900
  124.9 2.1 copy-start.10
  126.9 0.6 copy-start.11
  154.3 1.3 copy-start
